TPU v7x, 256 devices: a whole 4x4x8 slice. The times are simulated.
256 devices in a mesh: gx: 32 (over z, y_hi, core), gy: 8 (over x, y_lo).
Axes of the slice: x: 4, y: 4 (y_hi: 2, y_lo: 2; y = y_hi * 2 + y_lo), z: 8, core: 2. Of those that a mesh axis runs over, the one named last changes fastest.
Arguments:
- row_cells: int32 [8, 32, 4096], P('gy', 'gx'), may hold values from 0 to 255
- col_cells: int32 [8, 32, 4096], P('gy', 'gx'), may hold values from 0 to 255
- fracs: float32 [2, 8, 32, 4096], P(None, 'gy', 'gx'), may hold values from 0 to 1
- counts: int32 [8, 32], P('gy', 'gx'), may hold values from 512 to 4096, as said below
- targets: float32 [8, 32, 4096], P('gy', 'gx'), may hold values from -18 to 18
- amplitude: float32 [2048, 8192], P('gy', 'gx'), may hold values from 0.5 to 2
- lengthscale: float32 [2], replicated, may hold values from 51.2 to 64
- ridge: float32 [1], replicated, may hold values from 0.5 to 2
Outputs:
- solution: float32 [8, 32, 4096], P('gy', 'gx')
- residual: float32 [8, 32, 4096], P('gy', 'gx')
- relative: float32 [1], replicated
Inputs may be any that keep to these rules, and one draw needn't show every extreme that they name: Slots 0 to counts - 1 of a tile are live; some tile holds 4096 live points.
All inputs are finite; a program needn't handle non-finite values.
Results may differ from a plain program's by a relative error of at most 0.0003.
Values sent between devices are 32-bit elements; how exact they have to be, the bound alone decides.
No kernel may reach another device: no remote copies, remote signals or barrier semaphores. Data moves between devices by JAX's collectives and lax.ppermute only.
A program may use at most 64 MiB of HBM per device.

v0:
```python
import jax
import jax.numpy as jnp
from jax import lax
from jax.experimental import pallas as pl
from jax.experimental.pallas import tpu as pltpu
from jax.sharding import PartitionSpec as P

f32 = jnp.float32
bf16 = jnp.bfloat16
HB = 128
T = 256
E = 264
L = 384
H = 144
K = E + 2 * H
STEP = 512
MM = (((1,), (0,)), ((), ()))
MT = (((1,), (1,)), ((), ()))


def dot(left, right, dims):
    return lax.dot_general(left, right, dims, preferred_element_type=f32)


def split(x):
    high = x.astype(bf16)
    return high, (x - high.astype(f32)).astype(bf16)


def cell_of(slot):
    return jnp.where(slot <= T + 1, slot, jnp.where(slot == T + 2, -1, -100000))


def cubic_weights(fraction):
    square = fraction * fraction
    cube = square * fraction
    return (
        -0.5 * cube + square - 0.5 * fraction,
        1.5 * cube - 2.5 * square + 1.0,
        -1.5 * cube + 2.0 * square + 0.5 * fraction,
        0.5 * cube - 0.5 * square,
    )


def stencil(cells, fraction, live=None):
    w = cubic_weights(fraction)
    if live is not None:
        w = tuple(x * live for x in w)
    d = cell_of(lax.broadcasted_iota(jnp.int32, (E, cells.shape[1]), 0)) - (cells - 1)
    return jnp.where(
        d == 0, w[0], jnp.where(d == 1, w[1], jnp.where(d == 2, w[2], jnp.where(d == 3, w[3], 0.0)))
    )


def stencils(i, rows, cols, fracs, count):
    at = pl.ds(i * STEP, STEP)
    slot = lax.broadcasted_iota(jnp.int32, (1, STEP), 1) + i * STEP
    live = (slot < count[0, 0]).astype(f32)
    return (
        at,
        live,
        stencil(rows[:, at], fracs[0:1, at], live),
        stencil(cols[:, at], fracs[1:2, at]),
    )


def add_spread(i, weighted, r, out, edge):
    ch, cl = split(weighted)
    rh, rl = split(r[:T])
    main = dot(ch, rh, MT) + dot(ch, rl, MT) + dot(cl, rh, MT)
    tail = r[T:]
    tail_high = tail.astype(bf16).astype(f32)
    pair = jnp.concatenate([tail_high, tail - tail_high], 0).astype(bf16)
    first = dot(ch, pair, MT)
    side = first[:, :8] + first[:, 8:] + dot(cl, pair, MT)[:, :8]
    if i == 0:
        edge[...] = jnp.zeros_like(edge)
        out[:, :T] = main
        edge[:, :8] = side
    else:
        out[:, :T] += main
        edge[:, :8] += side


def pick_parts(g):
    gh, gl = split(g[:, :T])
    tail = g[:, T : T + 8]
    tail_high = tail.astype(bf16).astype(f32)
    tail_low = tail - tail_high
    pack = jnp.concatenate([tail_high, tail_high, tail_low, jnp.zeros_like(tail)], 1).astype(bf16)
    return gh, gl, pack


def pick(parts, c, r):
    gh, gl, pack = parts
    ch, cl = split(c[:T])
    tail = c[T:]
    tail_high = tail.astype(bf16).astype(f32)
    tall = jnp.concatenate([tail_high, tail - tail_high, tail_high, jnp.zeros_like(tail)], 0)
    value = dot(gh, ch, MM) + dot(gh, cl, MM) + dot(gl, ch, MM) + dot(pack, tall.astype(bf16), MM)
    return jnp.sum(value * r, axis=0, keepdims=True)


def write_slabs(x, even, far, near):
    low = jnp.concatenate([x[: H - 8], x[T:E]], 0)
    high = x[E - H : E]
    far[:H] = jnp.where(even, low, high)
    near[:H] = jnp.where(even, high, low)


def edge_rows(x):
    row = lax.broadcasted_iota(jnp.int32, (8, x.shape[1]), 0)
    return jnp.where(row < 2, x[0:8], jnp.broadcast_to(x[T - 1 : T], (8, x.shape[1])))


def outside_rows(even, far, near):
    row = lax.broadcasted_iota(jnp.int32, far.shape, 0)
    before = jnp.where(even, far, near)
    after = jnp.where(even, near, far)
    return jnp.where(row < 2, after, jnp.where(row == 2, before, 0.0))


def smooth_by(bands, x):
    high, low = split(x)
    return dot(bands[0], high, MM) + dot(bands[0], low, MM) + dot(bands[1], high, MM)


def band(even, scale, high, low):
    out = cell_of(lax.broadcasted_iota(jnp.int32, (E, K), 0))
    k = lax.broadcasted_iota(jnp.int32, (E, K), 1)
    is_far = jnp.logical_and(k >= E, k < E + H)
    from_before = is_far == even
    j = jnp.where(k < E, k, jnp.where(is_far, k - E, k - E - H))
    slab = jnp.where(jnp.logical_or(from_before, j >= H - 8), j + (E - H), j)
    cell = cell_of(jnp.where(k < E, k, slab))
    source = jnp.where(k < E, cell, jnp.where(from_before, cell - T, cell + T))
    d = jnp.abs(source - out)
    distance = d.astype(f32)
    value = jnp.where(
        jnp.logical_and(d <= HB, out >= -1),
        jnp.exp(-distance * distance / (2.0 * scale * scale)),
        0.0,
    )
    high[...], low[...] = split(value)


def bands_kernel(place, scales, xh, xl, yh, yl):
    band(place[0] == 0, scales[1], xh, xl)
    band(place[1] == 0, scales[0], yh, yl)


def spread_kernel(rows, cols, fracs, count, targets, out, right, edge):
    for i in range(rows.shape[1] // STEP):
        at, live, r, c = stencils(i, rows, cols, fracs, count)
        vector = targets[:, at] * live
        right[:, at] = vector
        add_spread(i, c * vector, r, out, edge)
    out[:, T:] = edge[...]


def first_slabs_kernel(place, spread, amplitude, far_edge, near_edge, scaled, across_scale, far, near):
    ends = outside_rows(place[1] == 0, far_edge[...], near_edge[...])
    wide = jnp.concatenate([amplitude[...], ends, jnp.zeros((L - E, T), f32)], 0)
    scale = jnp.transpose(wide)
    across_scale[...] = scale
    scaled[:T] = spread[:T] * scale
    scaled[T:] = spread[T:]
    write_slabs(scaled[...], place[0] == 0, far, near)
    edges = edge_rows(scale)
    far[H:] = edges
    near[H:] = edges


def across_body(place, scaled, scale, ends, far, near, bands, across, far_out, near_out):
    edges = edge_rows(scale)
    field = jnp.concatenate(
        [
            scaled[:T],
            scaled[T:] * ends,
            far[: H - 8],
            far[H - 8 : H] * edges,
            near[: H - 8],
            near[H - 8 : H] * edges,
        ],
        0,
    )
    smoothed = smooth_by(bands, field)
    turned = jnp.transpose(jnp.concatenate([smoothed, jnp.zeros((L - E, L), f32)], 0))[:E]
    across[...] = turned
    write_slabs(turned, place[1] == 0, far_out, near_out)


def first_across_kernel(place, scaled, scale, far, near, xh, xl, across, far_out, near_out, ends, grid_scale):
    outside = outside_rows(place[0] == 0, far[H:], near[H:])
    ends[...] = outside
    whole = jnp.concatenate([scale[...], outside, jnp.zeros((L - E, L), f32)], 0)
    grid_scale[...] = jnp.transpose(whole)[:E]
    across_body(
        place, scaled[...], scale[...], outside, far[...], near[...], (xh[...], xl[...]), across, far_out, near_out
    )


def across_kernel(place, scaled, scale, ends, far, near, xh, xl, across, far_out, near_out):
    across_body(
        place, scaled[...], scale[...], ends[...], far[...], near[...], (xh[...], xl[...]), across, far_out, near_out
    )


def grid_parts(across, far, near, yh, yl, grid_scale):
    field = jnp.concatenate([across[...], far[...], near[...]], 0)
    return pick_parts(smooth_by((yh[...], yl[...]), field) * grid_scale[...])


def middle_kernel(
    place, count, across, far, near, yh, yl, grid_scale, rows, cols, fracs, scale,
    image, scaled, far_out, near_out, edge,
):
    parts = grid_parts(across, far, near, yh, yl, grid_scale)
    for i in range(rows.shape[1] // STEP):
        at, _, r, c = stencils(i, rows, cols, fracs, count)
        value = pick(parts, c, r)
        image[:, at] = value
        add_spread(i, c * value, r, scaled, edge)
    scaled[:, T:] = edge[...]
    scaled[:T] = scaled[:T] * scale[...]
    write_slabs(scaled[...], place[0] == 0, far_out, near_out)


def last_kernel(
    count, across, far, near, yh, yl, grid_scale, rows, cols, fracs, right, image,
    image_two, sums,
):
    parts = grid_parts(across, far, near, yh, yl, grid_scale)
    for i in range(rows.shape[1] // STEP):
        at, _, r, c = stencils(i, rows, cols, fracs, count)
        image_two[:, at] = pick(parts, c, r)
    b, v, w = right[...], image[...], image_two[...]
    lane = lax.broadcasted_iota(jnp.int32, (1, 128), 1)
    total = jnp.zeros((1, 128), f32)
    for i, product in enumerate((b * b, b * v, v * v, v * w, w * w)):
        total = jnp.where(lane == i, jnp.sum(product, axis=1, keepdims=True), total)
    sums[...] = total


def finish_kernel(ridge, parts, right, image, image_two, solution_out, residual_out, relative_out):
    total = jnp.sum(parts[...], axis=0, keepdims=True)
    bb, bv, vv, vw, ww = (total[:, i : i + 1] for i in range(5))
    rho = ridge[0]
    b_image = bv + rho * bb
    one = bb / b_image
    keep = 1.0 - one * rho
    mid = keep * keep * bb - 2.0 * keep * one * bv + one * one * vv
    curve = keep * keep * bv - 2.0 * keep * one * vv + one * one * vw
    ratio = mid / bb
    two = mid / (curve + rho * mid - ratio * mid / one)
    side = keep + ratio
    on_b = keep - two * rho * side
    on_v = -one - two * (side - rho * one)
    on_w = two * one
    b, v, w = right[...], image[...], image_two[...]
    solution_out[...] = (one + two * side) * b - (two * one) * v
    residual_out[...] = on_b * b + on_v * v + on_w * w
    end = (
        on_b * on_b * bb
        + 2.0 * on_b * on_v * bv
        + (on_v * on_v + 2.0 * on_b * on_w) * vv
        + 2.0 * on_v * on_w * vw
        + on_w * on_w * ww
    )
    relative_out[...] = jnp.broadcast_to(end / bb, relative_out.shape)


def call(kernel, outs, args, scalars, scratch=(), mib=20, flops=0):
    vmem = pl.BlockSpec(memory_space=pltpu.VMEM)
    smem = pl.BlockSpec(memory_space=pltpu.SMEM)
    shapes = tuple(jax.ShapeDtypeStruct(shape, dtype) for shape, dtype in outs)
    return pl.pallas_call(
        kernel,
        out_shape=shapes,
        in_specs=[smem if i in scalars else vmem for i in range(len(args))],
        out_specs=tuple(vmem for _ in outs),
        scratch_shapes=list(scratch),
        compiler_params=pltpu.CompilerParams(vmem_limit_bytes=mib << 20),
        cost_estimate=pl.CostEstimate(flops=flops, bytes_accessed=1 << 20, transcendentals=0),
    )(*args)


def solution(mesh):
    gx, gy = mesh.axis_names

    def pairs(axis):
        count = mesh.shape[axis]
        near = [(i, i ^ 1) for i in range(count)]
        far = [(i, (i + 1) % count if i % 2 else (i - 1) % count) for i in range(count)]
        return far, near

    def swap(axis, far, near):
        far_to, near_to = pairs(axis)
        return lax.ppermute(far, axis, far_to), lax.ppermute(near, axis, near_to)

    def shards(row_cells, col_cells, fracs, counts, targets, amplitude, lengthscale, ridge):
        n = targets.shape[2]
        rows, cols = row_cells.reshape(1, n), col_cells.reshape(1, n)
        fracs = fracs.reshape(2, n)
        place = jnp.stack([lax.axis_index(gx) % 2, lax.axis_index(gy) % 2]).astype(jnp.int32)
        edge = pltpu.VMEM((E, L - T), f32)
        vector = ((1, n), f32)
        grid = ((E, L), f32)
        slab = ((H, L), f32)
        tall = ((H + 8, L), f32)
        band_part = ((E, K), bf16)

        ends = jnp.concatenate([amplitude[0:2], amplitude[T - 1 : T], jnp.zeros((5, T), f32)], 0)
        far_end, near_end = swap(gy, ends, ends)
        xh, xl, yh, yl = call(bands_kernel, (band_part,) * 4, (place, lengthscale), (0, 1))
        spread, right = call(
            spread_kernel,
            (grid, vector),
            (rows, cols, fracs, counts, targets.reshape(1, n)),
            (3,),
            (edge,),
            flops=6 << 28,
        )
        scaled, scale, far, near = call(
            first_slabs_kernel,
            (grid, ((T, L), f32), tall, tall),
            (place, spread, amplitude, far_end, near_end),
            (0,),
        )
        far, near = swap(gx, far, near)
        across, far, near, outside, grid_scale = call(
            first_across_kernel,
            (grid, slab, slab, ((8, L), f32), grid),
            (place, scaled, scale, far, near, xh, xl),
            (0,),
        )
        far, near = swap(gy, far, near)
        image, scaled, far, near = call(
            middle_kernel,
            (vector, grid, slab, slab),
            (place, counts, across, far, near, yh, yl, grid_scale, rows, cols, fracs, scale),
            (0, 1),
            (edge,),
        )
        far, near = swap(gx, far, near)
        across, far, near = call(
            across_kernel,
            (grid, slab, slab),
            (place, scaled, scale, outside, far, near, xh, xl),
            (0,),
        )
        far, near = swap(gy, far, near)
        image_two, sums = call(
            last_kernel,
            (vector, ((1, 128), f32)),
            (counts, across, far, near, yh, yl, grid_scale, rows, cols, fracs, right, image),
            (0,),
        )
        devices = mesh.size
        copies = jnp.broadcast_to(sums[None], (devices, 1, 128))
        parts = lax.all_to_all(copies, (gx, gy), 0, 0).reshape(devices, 128)
        out, residual, relative = call(
            finish_kernel,
            (vector, vector, ((1, 128), f32)),
            (ridge, parts, right, image, image_two),
            (0,),
        )
        return out.reshape(1, 1, n), residual.reshape(1, 1, n), relative[0, :1]

    tiles = P(gy, gx, None)
    return jax.shard_map(
        shards,
        mesh=mesh,
        in_specs=(tiles, tiles, P(None, gy, gx, None), P(gy, gx), tiles, P(gy, gx), P(), P()),
        out_specs=(tiles, tiles, P()),
        check_vma=False,
    )
```

profile of v0, /device:TPU:1, one launch (start us, length us, event | category | flops | bytes accessed | tf_op | source)
XLA Modules:
  0.0 103.1 jit_solution(1338832491700908428)
XLA Ops:
  0.6 0.7 slice.10
  1.3 0.0 slice-start
  1.3 0.0 copy-start.5
  1.3 0.1 pad.2.clone
  1.4 0.6 slice-done
  2.0 0.1 maximum_maximum_fusion
  2.1 4.3 %collective-permute-start = (f32[8,256]{1,0:T(8,128)S(1)}, f32[8,256]{1,0:T(8,128)S(1)}, u32[]{:S(2)}, u32[]{:S(2)}) collective-permute-start(f32[8,256]{1,0:T(8,128)S(1)} %maximum_maximum_fusion), channel_id=1, source_target_pairs={{0,7},{1,2},{2,1},{3,4},{4,3},{5,6},{6,5},{7,0},{8,15},{9,10},{10,... | collective-permute-start | bytes 24584 | tf_op jit(solution)/shard_map/ppermute | solution.py:299
  6.4 0.0 collective-permute-start.1
  6.4 0.0 copy-done.5
  6.4 0.0 copy-start.2
  6.4 0.0 copy-start.3
  6.5 0.0 copy-start.1
  7.2 0.0 copy-done.2
  7.2 0.0 copy-done.3
  7.2 0.0 copy-done.1
  7.2 0.0 copy-start
  7.2 5.1 %shard_map.103 = (f32[264,384]{1,0:T(8,128)S(1)}, f32[1,4096]{1,0:T(1,128)S(1)}) custom-call(s32[1,4096]{1,0:T(1,128)S(1)} %bitcast.18, s32[1,4096]{1,0:T(1,128)S(1)} %bitcast.21, f32[2,4096]{1,0:T(2,128)S(1)} %bitcast.15, s32[1,1]{1,0:T(1,128)S(6)} %copy.14.count, f32[1,4096]{1,0:T(1,128)S(1)} %bitcast.25), custom_call_target="tpu_custom_call" | custom-call | flops 1610612736 | bytes 1048576 | tf_op jit(solution)/shard_map/pallas_call | solution.py:277
  12.3 0.1 pad_add_fusion.place
  12.3 0.0 collective-permute-done.far_edge
  12.3 0.0 collective-permute-done.1.near_edge
  12.3 0.0 copy-done
  12.3 0.7 shard_map.104
  13.1 0.0 copy-start.4
  13.1 3.5 %collective-permute-start.2 = (f32[152,384]{1,0:T(8,128)S(1)}, f32[152,384]{1,0:T(8,128)S(1)}, u32[]{:S(2)}, u32[]{:S(2)}) collective-permute-start(f32[152,384]{1,0:T(8,128)S(1)} %get-tuple-element.33), channel_id=1, source_target_pairs={{0,248},{8,16},{16,8},{24,32},{32,24},{40,48},{48,40},{56,64},{64,... | collective-permute-start | bytes 700424 | tf_op jit(solution)/shard_map/ppermute | solution.py:299
  16.6 4.8 %collective-permute-start.3 = (f32[152,384]{1,0:T(8,128)S(1)}, f32[152,384]{1,0:T(8,128)S(1)}, u32[]{:S(2)}, u32[]{:S(2)}) collective-permute-start(f32[152,384]{1,0:T(8,128)S(1)} %get-tuple-element.34), channel_id=1, source_target_pairs={{0,8},{8,0},{16,24},{24,16},{32,40},{40,32},{48,56},{56,48},{64,72... | collective-permute-start | bytes 700424 | tf_op jit(solution)/shard_map/ppermute | solution.py:299
  21.5 0.0 copy-done.4
  21.5 1.2 %shard_map.105 = (bf16[264,552]{1,0:T(8,128)(2,1)S(1)}, bf16[264,552]{1,0:T(8,128)(2,1)S(1)}, bf16[264,552]{1,0:T(8,128)(2,1)S(1)}, bf16[264,552]{1,0:T(8,128)(2,1)S(1)}) custom-call(s32[2]{0:T(128)S(1)} %pad_add_fusion.place, f32[2]{0:T(128)S(1)} %copy-done.4), custom_call_target="tpu_custom_call" | custom-call | bytes 1048576 | tf_op jit(solution)/shard_map/pallas_call | solution.py:277
  22.7 0.0 collective-permute-done.2.far
  22.7 0.0 collective-permute-done.3.near
  22.7 1.5 %shard_map.106 = (f32[264,384]{1,0:T(8,128)S(1)}, f32[144,384]{1,0:T(8,128)S(1)}, f32[144,384]{1,0:T(8,128)S(1)}, f32[8,384]{1,0:T(8,128)S(1)}, f32[264,384]{1,0:T(8,128)S(1)}) custom-call(s32[2]{0:T(128)S(1)} %pad_add_fusion.place, f32[264,384]{1,0:T(8,128)S(1)} %get-tuple-element.31.scaled, f32[256,384]{1,0:T(8,128)S(1)} %get-tuple-element.32.scale, ...), custom_call_target="tpu_custom_call" | custom-call | bytes 1048576 | tf_op jit(solution)/shard_map/pallas_call | solution.py:277
  24.2 1.2 %collective-permute-start.4 = (f32[144,384]{1,0:T(8,128)S(1)}, f32[144,384]{1,0:T(8,128)S(1)}, u32[]{:S(2)}, u32[]{:S(2)}) collective-permute-start(f32[144,384]{1,0:T(8,128)S(1)} %get-tuple-element.38), channel_id=1, source_target_pairs={{0,7},{1,2},{2,1},{3,4},{4,3},{5,6},{6,5},{7,0},{8,15},{9,10},{10,... | collective-permute-start | bytes 663560 | tf_op jit(solution)/shard_map/ppermute | solution.py:299
  25.4 0.5 collective-permute-start.5
  25.9 5.4 %collective-permute-done.4.far = f32[144,384]{1,0:T(8,128)S(1)} collective-permute-done((f32[144,384]{1,0:T(8,128)S(1)}, f32[144,384]{1,0:T(8,128)S(1)}, u32[]{:S(2)}, u32[]{:S(2)}) %collective-permute-start.4) | collective-permute-done | bytes 221216 | tf_op jit(solution)/shard_map/ppermute | solution.py:299
  31.3 5.2 %collective-permute-done.5.near = f32[144,384]{1,0:T(8,128)S(1)} collective-permute-done((f32[144,384]{1,0:T(8,128)S(1)}, f32[144,384]{1,0:T(8,128)S(1)}, u32[]{:S(2)}, u32[]{:S(2)}) %collective-permute-start.5) | collective-permute-done | bytes 221216 | tf_op jit(solution)/shard_map/ppermute | solution.py:299
  36.5 10.3 %shard_map.107 = (f32[1,4096]{1,0:T(1,128)S(1)}, f32[264,384]{1,0:T(8,128)S(1)}, f32[144,384]{1,0:T(8,128)S(1)}, f32[144,384]{1,0:T(8,128)S(1)}) custom-call(s32[2]{0:T(128)S(1)} %pad_add_fusion.place, s32[1,1]{1,0:T(1,128)S(6)} %copy.14.count, f32[264,384]{1,0:T(8,128)S(1)} %get-tuple-element.37.across, f32[144,384]{1,0:T(8,128)S(1)} %collective-permute-done.4.far, ...), custom_call_target="tpu_custom_call" | custom-call | bytes 1048576 | tf_op jit(solution)/shard_map/pallas_call | solution.py:277
  46.8 3.2 %collective-permute-start.6 = (f32[144,384]{1,0:T(8,128)S(1)}, f32[144,384]{1,0:T(8,128)S(1)}, u32[]{:S(2)}, u32[]{:S(2)}) collective-permute-start(f32[144,384]{1,0:T(8,128)S(1)} %get-tuple-element.45), channel_id=1, source_target_pairs={{0,248},{8,16},{16,8},{24,32},{32,24},{40,48},{48,40},{56,64},{64,... | collective-permute-start | bytes 663560 | tf_op jit(solution)/shard_map/ppermute | solution.py:299
  49.9 6.1 %collective-permute-start.7 = (f32[144,384]{1,0:T(8,128)S(1)}, f32[144,384]{1,0:T(8,128)S(1)}, u32[]{:S(2)}, u32[]{:S(2)}) collective-permute-start(f32[144,384]{1,0:T(8,128)S(1)} %get-tuple-element.46), channel_id=1, source_target_pairs={{0,8},{8,0},{16,24},{24,16},{32,40},{40,32},{48,56},{56,48},{64,72... | collective-permute-start | bytes 663560 | tf_op jit(solution)/shard_map/ppermute | solution.py:299
  56.0 0.0 collective-permute-done.6.far
  56.0 1.1 %collective-permute-done.7.near = f32[144,384]{1,0:T(8,128)S(1)} collective-permute-done((f32[144,384]{1,0:T(8,128)S(1)}, f32[144,384]{1,0:T(8,128)S(1)}, u32[]{:S(2)}, u32[]{:S(2)}) %collective-permute-start.7) | collective-permute-done | bytes 221216 | tf_op jit(solution)/shard_map/ppermute | solution.py:299
  57.1 1.5 %shard_map.108 = (f32[264,384]{1,0:T(8,128)S(1)}, f32[144,384]{1,0:T(8,128)S(1)}, f32[144,384]{1,0:T(8,128)S(1)}) custom-call(s32[2]{0:T(128)S(1)} %pad_add_fusion.place, f32[264,384]{1,0:T(8,128)S(1)} %get-tuple-element.43.scaled, f32[256,384]{1,0:T(8,128)S(1)} %get-tuple-element.32.scale, f32[8,384]{1,0:T(8,128)S(1)} %get-tuple-element.44.ends, ...), custom_call_target="tpu_custom_call" | custom-call | bytes 1048576 | tf_op jit(solution)/shard_map/pallas_call | solution.py:277
  58.6 1.5 %collective-permute-start.8 = (f32[144,384]{1,0:T(8,128)S(1)}, f32[144,384]{1,0:T(8,128)S(1)}, u32[]{:S(2)}, u32[]{:S(2)}) collective-permute-start(f32[144,384]{1,0:T(8,128)S(1)} %get-tuple-element.48), channel_id=1, source_target_pairs={{0,7},{1,2},{2,1},{3,4},{4,3},{5,6},{6,5},{7,0},{8,15},{9,10},{10,... | collective-permute-start | bytes 663560 | tf_op jit(solution)/shard_map/ppermute | solution.py:299
  60.1 0.0 collective-permute-start.9
  60.1 5.6 %collective-permute-done.8.far = f32[144,384]{1,0:T(8,128)S(1)} collective-permute-done((f32[144,384]{1,0:T(8,128)S(1)}, f32[144,384]{1,0:T(8,128)S(1)}, u32[]{:S(2)}, u32[]{:S(2)}) %collective-permute-start.8) | collective-permute-done | bytes 221216 | tf_op jit(solution)/shard_map/ppermute | solution.py:299
  65.7 5.7 %collective-permute-done.9.near = f32[144,384]{1,0:T(8,128)S(1)} collective-permute-done((f32[144,384]{1,0:T(8,128)S(1)}, f32[144,384]{1,0:T(8,128)S(1)}, u32[]{:S(2)}, u32[]{:S(2)}) %collective-permute-start.9) | collective-permute-done | bytes 221216 | tf_op jit(solution)/shard_map/ppermute | solution.py:299
  71.4 4.8 %shard_map.109 = (f32[1,4096]{1,0:T(1,128)S(1)}, f32[1,128]{1,0:T(1,128)S(1)}) custom-call(s32[1,1]{1,0:T(1,128)S(6)} %copy.14.count, f32[264,384]{1,0:T(8,128)S(1)} %get-tuple-element.47.across, f32[144,384]{1,0:T(8,128)S(1)} %collective-permute-done.8.far, f32[144,384]{1,0:T(8,128)S(1)} %collective-permute-done.9.near, ...), custom_call_target="tpu_custom_call" | custom-call | bytes 1048576 | tf_op jit(solution)/shard_map/pallas_call | solution.py:277
  76.2 0.7 broadcast_in_dim.13
  77.0 12.0 %all-to-all-start = ((f32[256,1,128]{2,1,0:T(1,128)}), f32[256,1,128]{2,1,0:T(1,128)S(1)}, u32[]{:S(2)}, u32[]{:S(2)}) async-start(f32[256,1,128]{2,1,0:T(1,128)} %broadcast_in_dim.13), calls=%async_computation | async-start | bytes 262144 | tf_op jit(solution)/shard_map/all_to_all | solution.py:361
  89.6 12.5 %all-to-all-done = f32[256,1,128]{2,1,0:T(1,128)S(1)} async-done(((f32[256,1,128]{2,1,0:T(1,128)}), f32[256,1,128]{2,1,0:T(1,128)S(1)}, u32[]{:S(2)}, u32[]{:S(2)}) %all-to-all-start) | async-done | bytes 131104 | tf_op jit(solution)/shard_map/all_to_all | solution.py:361
  102.2 0.9 shard_map.110
  (2 shorter events, 0.0 us)
Async XLA Ops:
  1.3 0.7 slice-start
  1.3 5.1 %copy-start.5 = (f32[2,1,1,4096]{3,2,1,0:T(1,128)S(1)}, f32[2,1,1,4096]{3,2,1,0:T(1,128)}, u32[]{:S(2)}) copy-start(f32[2,1,1,4096]{3,2,1,0:T(1,128)} %param.10) | copy-start | bytes 98308
  2.1 10.3 %collective-permute-start = (f32[8,256]{1,0:T(8,128)S(1)}, f32[8,256]{1,0:T(8,128)S(1)}, u32[]{:S(2)}, u32[]{:S(2)}) collective-permute-start(f32[8,256]{1,0:T(8,128)S(1)} %maximum_maximum_fusion), channel_id=1, source_target_pairs={{0,7},{1,2},{2,1},{3,4},{4,3},{5,6},{6,5},{7,0},{8,15},{9,10},{10,... | collective-permute-start | bytes 24584 | tf_op jit(solution)/shard_map/ppermute | solution.py:299
  6.4 5.9 %collective-permute-start.1 = (f32[8,256]{1,0:T(8,128)S(1)}, f32[8,256]{1,0:T(8,128)S(1)}, u32[]{:S(2)}, u32[]{:S(2)}) collective-permute-start(f32[8,256]{1,0:T(8,128)S(1)} %maximum_maximum_fusion), channel_id=1, source_target_pairs={{0,1},{1,0},{2,3},{3,2},{4,5},{5,4},{6,7},{7,6},{8,9},{9,8},{10,11... | collective-permute-start | bytes 24584 | tf_op jit(solution)/shard_map/ppermute | solution.py:299
  6.4 0.7 copy-start.2
  6.4 0.7 copy-start.3
  6.5 0.7 copy-start.1
  7.2 5.2 %copy-start = (f32[256,256]{1,0:T(8,128)S(1)}, f32[256,256]{1,0:T(8,128)}, u32[]{:S(2)}) copy-start(f32[256,256]{1,0:T(8,128)} %amplitude.1) | copy-start | bytes 786436
  13.1 8.4 %copy-start.4 = (f32[2]{0:T(128)S(1)}, f32[2]{0:T(128)}, u32[]{:S(2)}) copy-start(f32[2]{0:T(128)} %scales.1) | copy-start | bytes 28
  13.1 9.6 %collective-permute-start.2 = (f32[152,384]{1,0:T(8,128)S(1)}, f32[152,384]{1,0:T(8,128)S(1)}, u32[]{:S(2)}, u32[]{:S(2)}) collective-permute-start(f32[152,384]{1,0:T(8,128)S(1)} %get-tuple-element.33), channel_id=1, source_target_pairs={{0,248},{8,16},{16,8},{24,32},{32,24},{40,48},{48,40},{56,64},{64,... | collective-permute-start | bytes 700424 | tf_op jit(solution)/shard_map/ppermute | solution.py:299
  16.6 6.0 %collective-permute-start.3 = (f32[152,384]{1,0:T(8,128)S(1)}, f32[152,384]{1,0:T(8,128)S(1)}, u32[]{:S(2)}, u32[]{:S(2)}) collective-permute-start(f32[152,384]{1,0:T(8,128)S(1)} %get-tuple-element.34), channel_id=1, source_target_pairs={{0,8},{8,0},{16,24},{24,16},{32,40},{40,32},{48,56},{56,48},{64,72... | collective-permute-start | bytes 700424 | tf_op jit(solution)/shard_map/ppermute | solution.py:299
  24.2 7.1 %collective-permute-start.4 = (f32[144,384]{1,0:T(8,128)S(1)}, f32[144,384]{1,0:T(8,128)S(1)}, u32[]{:S(2)}, u32[]{:S(2)}) collective-permute-start(f32[144,384]{1,0:T(8,128)S(1)} %get-tuple-element.38), channel_id=1, source_target_pairs={{0,7},{1,2},{2,1},{3,4},{4,3},{5,6},{6,5},{7,0},{8,15},{9,10},{10,... | collective-permute-start | bytes 663560 | tf_op jit(solution)/shard_map/ppermute | solution.py:299
  25.4 11.1 %collective-permute-start.5 = (f32[144,384]{1,0:T(8,128)S(1)}, f32[144,384]{1,0:T(8,128)S(1)}, u32[]{:S(2)}, u32[]{:S(2)}) collective-permute-start(f32[144,384]{1,0:T(8,128)S(1)} %get-tuple-element.39), channel_id=1, source_target_pairs={{0,1},{1,0},{2,3},{3,2},{4,5},{5,4},{6,7},{7,6},{8,9},{9,8},{10,11... | collective-permute-start | bytes 663560 | tf_op jit(solution)/shard_map/ppermute | solution.py:299
  46.8 9.3 %collective-permute-start.6 = (f32[144,384]{1,0:T(8,128)S(1)}, f32[144,384]{1,0:T(8,128)S(1)}, u32[]{:S(2)}, u32[]{:S(2)}) collective-permute-start(f32[144,384]{1,0:T(8,128)S(1)} %get-tuple-element.45), channel_id=1, source_target_pairs={{0,248},{8,16},{16,8},{24,32},{32,24},{40,48},{48,40},{56,64},{64,... | collective-permute-start | bytes 663560 | tf_op jit(solution)/shard_map/ppermute | solution.py:299
  49.9 7.2 %collective-permute-start.7 = (f32[144,384]{1,0:T(8,128)S(1)}, f32[144,384]{1,0:T(8,128)S(1)}, u32[]{:S(2)}, u32[]{:S(2)}) collective-permute-start(f32[144,384]{1,0:T(8,128)S(1)} %get-tuple-element.46), channel_id=1, source_target_pairs={{0,8},{8,0},{16,24},{24,16},{32,40},{40,32},{48,56},{56,48},{64,72... | collective-permute-start | bytes 663560 | tf_op jit(solution)/shard_map/ppermute | solution.py:299
  58.6 7.1 %collective-permute-start.8 = (f32[144,384]{1,0:T(8,128)S(1)}, f32[144,384]{1,0:T(8,128)S(1)}, u32[]{:S(2)}, u32[]{:S(2)}) collective-permute-start(f32[144,384]{1,0:T(8,128)S(1)} %get-tuple-element.48), channel_id=1, source_target_pairs={{0,7},{1,2},{2,1},{3,4},{4,3},{5,6},{6,5},{7,0},{8,15},{9,10},{10,... | collective-permute-start | bytes 663560 | tf_op jit(solution)/shard_map/ppermute | solution.py:299
  60.1 11.3 %collective-permute-start.9 = (f32[144,384]{1,0:T(8,128)S(1)}, f32[144,384]{1,0:T(8,128)S(1)}, u32[]{:S(2)}, u32[]{:S(2)}) collective-permute-start(f32[144,384]{1,0:T(8,128)S(1)} %get-tuple-element.49), channel_id=1, source_target_pairs={{0,1},{1,0},{2,3},{3,2},{4,5},{5,4},{6,7},{7,6},{8,9},{9,8},{10,11... | collective-permute-start | bytes 663560 | tf_op jit(solution)/shard_map/ppermute | solution.py:299
  77.0 25.2 %all-to-all-start = ((f32[256,1,128]{2,1,0:T(1,128)}), f32[256,1,128]{2,1,0:T(1,128)S(1)}, u32[]{:S(2)}, u32[]{:S(2)}) async-start(f32[256,1,128]{2,1,0:T(1,128)} %broadcast_in_dim.13), calls=%async_computation | async-start | bytes 262144 | tf_op jit(solution)/shard_map/all_to_all | solution.py:361
where the time goes:
time: 103 us
  starting transfers between devices  37.2 us (36%)
  waiting for transfers between devices  35.6 us (35%)
  Pallas kernels  26 us (25%)
  local copies, waits for them, and re-layouts  2.18 us (2%)
  between operations  2.08 us (2%)
    pallas_call x8, Pallas kernels, call(): pl.pallas_call(kernel, out_shape=shapes, in_specs=[smem if i in scalars e...  26 us
    ppermute x10, starting transfers between devices, swap(): return (lax.ppermute(far, axis, far_to), lax.ppermute(near, axis, near_to))  25.2 us
    ppermute x10, waiting for transfers between devices, swap(): return (lax.ppermute(far, axis, far_to), lax.ppermute(near, axis, near_to))  23 us
    all_to_all x1, waiting for transfers between devices, shards(): parts = lax.all_to_all(copies, (gx, gy), 0, 0).reshape(devices, 128)  12.5 us
    all_to_all x1, starting transfers between devices, shards(): parts = lax.all_to_all(copies, (gx, gy), 0, 0).reshape(devices, 128)  12 us
  transfers between devices with their start and end apart: 11, of which 6 were waited for; matrix products, arithmetic and copies ran while one was open for 0% of the time, Pallas kernels for 6%

commit v1 on v0

v1 whole, which is shorter than its diff:
```python
import jax
import jax.numpy as jnp
from jax import lax
from jax.experimental import pallas as pl
from jax.experimental.pallas import tpu as pltpu
from jax.sharding import PartitionSpec as P

f32 = jnp.float32
bf16 = jnp.bfloat16
HB = 128
T = 256
HALF = T // 2
E = T + 8
TALL = T + 16
SLAB = HALF + 16
FIELD = 2 * T + 24
K = 2 * T + 128
STEP = 512
MM = (((1,), (0,)), ((), ()))
MT = (((1,), (1,)), ((), ()))


def dot(left, right, dims):
    return lax.dot_general(left, right, dims, preferred_element_type=f32)


def split(x):
    high = x.astype(bf16)
    return high, (x - high.astype(f32)).astype(bf16)


def split_rows(x):
    high = x.astype(bf16).astype(f32)
    return jnp.concatenate([high, x - high], 0).astype(bf16)


def iota(shape, dim):
    return lax.broadcasted_iota(jnp.int32, shape, dim)


def cell_of(slot):
    return jnp.where(slot <= T + 1, slot, jnp.where(slot == T + 2, -1, -9999))


def cubic_weights(fraction):
    square = fraction * fraction
    cube = square * fraction
    return (
        -0.5 * cube + square - 0.5 * fraction,
        1.5 * cube - 2.5 * square + 1.0,
        -1.5 * cube + 2.0 * square + 0.5 * fraction,
        0.5 * cube - 0.5 * square,
    )


def slots(first, count, wrap):
    cell = cell_of(first + iota((count, 128), 0) % wrap).astype(jnp.int16)
    return jnp.concatenate([cell] * (STEP // 128), 1)


def place(cell, targets, weights):
    hits = [cell == target for target in targets]
    out = []
    for group in weights:
        value = jnp.zeros(cell.shape, bf16)
        for hit, weight in zip(hits, group):
            value = jnp.where(hit, jnp.broadcast_to(weight, cell.shape), value)
        out.append(value)
    return out


def touched(cells):
    return [(cells + (j - 1)).astype(jnp.int16) for j in range(4)]


def weight_parts(fraction, factor=None):
    pairs = [split(w if factor is None else w * factor) for w in cubic_weights(fraction)]
    return [high for high, _ in pairs], [low for _, low in pairs]


class Rows:
    def __init__(self):
        self.main = slots(0, T, T)
        self.tail = slots(T, 16, 16)
        self.twice = slots(T, 16, 8)
        self.upper = iota((16, STEP), 0) < 8

    def pair(self, targets, weights):
        high, low = place(self.twice, targets, weights)
        return jnp.where(self.upper, high.astype(f32), low.astype(f32)).astype(bf16)


def add_spread(i, rows, r_main, r_pair, targets, weights, out, edge):
    main, tail = place(rows.main, targets, weights), place(rows.tail, targets, weights)
    high, low = (jnp.concatenate([x, y], 0) for x, y in zip(main, tail))
    inner = dot(high, r_main[0], MT) + dot(high, r_main[1], MT) + dot(low, r_main[0], MT)
    first = dot(r_pair, high, MT)
    side = first[:8] + first[8:] + dot(r_pair, low, MT)[:8]
    if i == 0:
        edge[...] = jnp.zeros_like(edge)
        out[...] = inner[:E]
        edge[:, :TALL] = side
    else:
        out[...] += inner[:E]
        edge[:, :TALL] += side


def pick(grid, c_main, c_pair, r):
    high, low, tail = grid
    pack = jnp.concatenate([c_pair, c_pair], 0)
    value = dot(high, c_main[0], MM) + dot(high, c_main[1], MM) + dot(low, c_main[0], MM)
    value = value + dot(tail, pack, MM)
    return jnp.sum(value * r, axis=0, keepdims=True)


def put(row, value, index, x):
    return jnp.where(row == index, jnp.broadcast_to(value, x.shape), x)


def group_low(x, tail, dim):
    row = iota(tail.shape, dim)
    at = (lambda i: x[i : i + 1]) if dim == 0 else (lambda i: x[:, i : i + 1])
    return put(row, at(HALF), 6, put(row, at(HALF + 1), 7, tail))


def group_high(x, tail, dim):
    row = iota(tail.shape, dim)
    at = (lambda i: x[i : i + 1]) if dim == 0 else (lambda i: x[:, i : i + 1])
    return put(row, at(HALF - 1), 7, tail)


def edge_rows(x):
    row = iota((8, x.shape[1]), 0)
    return jnp.where(row < 2, x[:8], jnp.broadcast_to(x[T - 1 : T], row.shape))


def outside_rows(even, far, near):
    row = iota(far.shape, 0)
    before = jnp.where(even, far, near)
    after = jnp.where(even, near, far)
    return jnp.where(row < 2, after, jnp.where(row == 2, before, 0.0))


def outside_lanes(even, far, near):
    lane = iota((8, 128), 1)
    before = jnp.where(even, far, near)
    after = jnp.where(even, near, far)
    last = jnp.broadcast_to(before[:, T - 1 : T], lane.shape)
    return jnp.where(lane < 2, after[:, :128], jnp.where(lane == 2, last, 0.0))


def column_slabs(even, main, edge, far, near):
    tail = main[T:]
    low_rows, high_rows = group_low(main, tail, 0), group_high(main, tail, 0)
    lanes = edge[:, T:]
    low_lanes, high_lanes = group_low(edge, lanes, 1), group_high(edge, lanes, 1)
    for ref, low, shift in ((far, even, 8), (near, jnp.logical_not(even), 16)):
        ref[:HALF] = jnp.where(low, main[:HALF], main[HALF:T])
        ref[HALF : HALF + 8] = jnp.where(low, low_rows, high_rows)
        ref[HALF + 8 : SLAB, :128] = jnp.where(low, edge[:, :HALF], edge[:, HALF:T])
        group = jnp.where(low, low_lanes, high_lanes)
        group = jnp.where(iota(group.shape, 1) < 8, group, 0.0)
        ref[HALF + 8 : SLAB, 128:] = pltpu.roll(group, shift, 1)


def row_slabs(even, main, group, tail, far, near):
    low_rows, high_rows = group_low(main, group, 0), group_high(main, group, 0)
    for ref, low in ((far, even), (near, jnp.logical_not(even))):
        ref[:HALF] = jnp.where(low, main[:HALF, :T], main[HALF:, :T])
        rows = jnp.where(low, low_rows, high_rows)
        ref[HALF : HALF + 8] = rows[:, :T]
        ref[HALF + 8 : SLAB, :128] = jnp.where(low, tail[:, :HALF], tail[:, HALF:])
        ref[HALF + 8 : SLAB, 128:] = rows[:, T:]


def smooth_by(bands, x):
    high, low = split(x)
    return dot(bands[0], high, MM) + dot(bands[0], low, MM) + dot(bands[1], high, MM)


def band(even, scale, high, low):
    out = cell_of(iota((E, K), 0))
    k = iota((E, K), 1)
    j = k - 2 * T
    is_own = jnp.logical_or(k < T, jnp.logical_and(j >= 0, j < 8))
    is_far = jnp.logical_or(
        jnp.logical_and(k >= T, k < T + HALF), jnp.logical_and(j >= 8, j < 16)
    )
    before = is_far == even
    g = j % 8
    extra = jnp.where(before, jnp.where(g == 7, HALF - 1, -9999), g + (HALF - 6))
    extra = jnp.where(jnp.logical_or(is_own, g < 6), -9999, extra)
    group = jnp.where(g < 3, cell_of(T + g), extra)
    inner = jnp.where(is_own, k, k % HALF + jnp.where(before, HALF, 0))
    cell = jnp.where(j < 0, inner, jnp.where(j < 24, group, -9999))
    source = jnp.where(is_own, cell, jnp.where(before, cell - T, cell + T))
    d = jnp.abs(source - out)
    distance = d.astype(f32)
    value = jnp.where(
        jnp.logical_and(d <= HB, out >= -1),
        jnp.exp(-distance * distance / (2.0 * scale * scale)),
        0.0,
    )
    high[...], low[...] = split(value)


def bands_kernel(spot, scales, xh, xl, yh, yl):
    band(spot[0] == 0, scales[1], xh, xl)
    band(spot[1] == 0, scales[0], yh, yl)


def fields(points, at):
    cells = [points[i : i + 1, at].astype(jnp.int32) for i in range(2)]
    return cells + [points[i : i + 1, at] for i in range(2, 6)]


def spread_kernel(points, out, edge):
    kinds = Rows()
    for i in range(points.shape[1] // STEP):
        at = pl.ds(i * STEP, STEP)
        rows, cols, row_fracs, col_fracs, live, vector = fields(points, at)
        r_at, r_weights = touched(rows), weight_parts(row_fracs, live)
        r_main = place(kinds.main, r_at, r_weights)
        r_pair = kinds.pair(r_at, r_weights)
        c_weights = weight_parts(col_fracs, vector)
        add_spread(i, kinds, r_main, r_pair, touched(cols), c_weights, out, edge)


def scaled_slabs(even, main, edge, turned, ends, main_out, edge_out, far, near):
    main_out[:T] = main[:T] * turned[...]
    main_out[T:] = main[T:]
    edge_out[:, :T] = edge[:, :T] * ends
    edge_out[:, T:] = edge[:, T:]
    column_slabs(even, main_out[...], edge_out[...], far, near)


def first_slabs_kernel(
    spot, main, edge, amplitude, far_ends, near_ends, main_out, edge_out, turned, ends, far, near
):
    row = iota((8, T), 0)
    far_rows, near_rows = (
        jnp.where(row < 2, x[:8], jnp.broadcast_to(x[15:], row.shape)) for x in (far_ends, near_ends)
    )
    ends[...] = outside_rows(spot[1] == 0, far_rows, near_rows)
    turned[...] = jnp.transpose(amplitude[...])
    scaled_slabs(
        spot[0] == 0, main[...], edge[...], turned, ends[...], main_out, edge_out, far, near
    )
    for ref in (far, near):
        ref[SLAB : SLAB + 8] = edge_rows(turned[...])
        ref[SLAB + 8 :] = ends[...]


def across_body(even_row, main, edge, turned, ends, outside, corner, far, near, bands, outs):
    row_out, group_out, tail_out, far_out, near_out = outs
    row = iota((8, T), 0)
    edges = jnp.where(row < 3, edge_rows(turned), 1.0)
    field = jnp.concatenate(
        [
            main[:T],
            far[:HALF],
            near[:HALF],
            main[T:] * outside,
            far[HALF : HALF + 8] * edges,
            near[HALF : HALF + 8] * edges,
        ],
        0,
    )
    smoothed = smooth_by((bands[0][:, :FIELD], bands[1][:, :FIELD]), field)
    lane = iota((8, 128), 1)
    g = lane % 8
    first, second = (jnp.broadcast_to(ends[:, i : i + 1], lane.shape) for i in (0, 1))
    third = jnp.broadcast_to(ends[:, T - 1 : T], lane.shape)
    factor = jnp.where(g == 0, first, jnp.where(g == 1, second, jnp.where(g == 2, third, 1.0)))
    factor = jnp.where(lane < 8, corner, factor)
    own = jnp.where(lane < 8, edge[:, T:], 0.0)
    groups = (own + far[HALF + 8 : SLAB, 128:] + near[HALF + 8 : SLAB, 128:]) * factor
    strip = jnp.concatenate(
        [edge[:, :T], far[HALF + 8 : SLAB, :128], near[HALF + 8 : SLAB, :128], groups], 1
    )
    pair = split_rows(strip)
    by_high = dot(pair, bands[0], MT)
    group = by_high[:8] + by_high[8:] + dot(pair, bands[1], MT)[:8]
    group = jnp.concatenate([group, jnp.zeros((8, 384 - E), f32)], 1)
    turned_back = jnp.transpose(jnp.concatenate([smoothed, jnp.zeros((384 - E, T), f32)], 0))
    row_out[...] = turned_back
    group_out[...] = group
    tail_out[...] = smoothed[T:]
    row_slabs(even_row, turned_back, group, smoothed[T:], far_out, near_out)


def first_across_kernel(
    spot, main, edge, amplitude, turned, ends, far, near, xh, xl,
    row_out, group_out, tail_out, far_out, near_out, outside, corner, scale, scale_tail,
):
    even = spot[0] == 0
    outside[...] = outside_rows(even, far[SLAB : SLAB + 8], near[SLAB : SLAB + 8])
    corner[...] = outside_lanes(even, far[SLAB + 8 :], near[SLAB + 8 :])
    scale[:T] = amplitude[...]
    scale[T:] = ends[...]
    wide = jnp.concatenate([outside[...], jnp.zeros((120, T), f32)], 0)
    scale_tail[:T] = jnp.transpose(wide)
    scale_tail[T:] = corner[...]
    across_body(
        spot[1] == 0, main[...], edge[...], turned[...], ends[...], outside[...], corner[...],
        far[...], near[...], (xh[...], xl[...]), (row_out, group_out, tail_out, far_out, near_out),
    )


def across_kernel(
    spot, main, edge, turned, ends, outside, corner, far, near, xh, xl,
    row_out, group_out, tail_out, far_out, near_out,
):
    across_body(
        spot[1] == 0, main[...], edge[...], turned[...], ends[...], outside[...], corner[...],
        far[...], near[...], (xh[...], xl[...]), (row_out, group_out, tail_out, far_out, near_out),
    )


def grid_parts(row, group, tail, far, near, yh, yl, scale, scale_tail):
    far_group, near_group = far[HALF : HALF + 8], near[HALF : HALF + 8]
    field = jnp.concatenate(
        [row[:, :T], far[:HALF], near[:HALF], group[:, :T], far_group, near_group], 0
    )
    main = smooth_by((yh[:, :FIELD], yl[:, :FIELD]), field) * scale[...]
    strip = jnp.concatenate(
        [tail[...], far[HALF + 8 : SLAB, :128], near[HALF + 8 : SLAB, :128]], 1
    )
    pair = split_rows(strip)
    by_high = dot(yh[:, : 2 * T], pair, MT)
    side = by_high[:, :8] + by_high[:, 8:] + dot(yl[:, : 2 * T], pair, MT)[:, :8]
    ends = jnp.concatenate(
        [group[:, T:], far[HALF + 8 : SLAB, 128:], near[HALF + 8 : SLAB, 128:]], 0
    )
    side = side + smooth_by((yh[:, 2 * T : FIELD], yl[:, 2 * T : FIELD]), ends)[:, :8]
    side = side * scale_tail[:, :8]
    high, low = split(main)
    side_high = side.astype(bf16).astype(f32)
    side_low = side - side_high
    zero = jnp.zeros_like(side)
    return high, low, jnp.concatenate([side_high, side_high, side_low, zero], 1).astype(bf16)


def stencil(cells, fraction, live):
    w = [x * live for x in cubic_weights(fraction)]
    d = cell_of(iota((E, STEP), 0)) - (cells - 1)
    return jnp.where(
        d == 0, w[0], jnp.where(d == 1, w[1], jnp.where(d == 2, w[2], jnp.where(d == 3, w[3], 0.0)))
    )


def weights_kernel(points, after, r_high, r_low, r_twice, r_all, c_high, c_low, c_twice):
    kinds = Rows()
    for i in range(points.shape[1] // STEP):
        at = pl.ds(i * STEP, STEP)
        rows, cols, row_fracs, col_fracs, live, _ = fields(points, at)
        r_all[:, at] = stencil(rows, row_fracs, live)
        r_at, r_weights = touched(rows), weight_parts(row_fracs, live)
        r_high[:, at], r_low[:, at] = place(kinds.main, r_at, r_weights)
        r_twice[:, at] = kinds.pair(r_at, r_weights)
        c_at, c_weights = touched(cols), weight_parts(col_fracs)
        c_high[:, at], c_low[:, at] = place(kinds.main, c_at, c_weights)
        c_twice[:, at] = kinds.pair(c_at, c_weights)


def middle_kernel(
    spot, row, group, tail, far, near, yh, yl, scale, scale_tail, points, r_high, r_low, r_twice,
    r_all, c_high, c_low, c_twice, turned, ends, image, main_out, edge_out, far_out, near_out, main, edge,
):
    grid = grid_parts(row, group, tail, far, near, yh, yl, scale, scale_tail)
    kinds = Rows()
    for i in range(points.shape[1] // STEP):
        at = pl.ds(i * STEP, STEP)
        value = pick(grid, (c_high[:, at], c_low[:, at]), c_twice[:, at], r_all[:, at])
        image[:, at] = value
    for i in range(points.shape[1] // STEP):
        at = pl.ds(i * STEP, STEP)
        _, cols, _, col_fracs, _, _ = fields(points, at)
        c_weights = weight_parts(col_fracs, image[:, at])
        r_main = r_high[:, at], r_low[:, at]
        add_spread(i, kinds, r_main, r_twice[:, at], touched(cols), c_weights, main, edge)
    scaled_slabs(
        spot[0] == 0, main[...], edge[...], turned, ends[...], main_out, edge_out, far_out, near_out
    )


def last_kernel(
    row, group, tail, far, near, yh, yl, scale, scale_tail, r_all, c_high, c_low, c_twice, points, image,
    image_two, sums,
):
    grid = grid_parts(row, group, tail, far, near, yh, yl, scale, scale_tail)
    for i in range(r_all.shape[1] // STEP):
        at = pl.ds(i * STEP, STEP)
        image_two[:, at] = pick(grid, (c_high[:, at], c_low[:, at]), c_twice[:, at], r_all[:, at])
    b, v, w = points[5:6], image[...], image_two[...]
    lane = iota((1, 128), 1)
    total = jnp.zeros((1, 128), f32)
    for i, product in enumerate((b * b, b * v, v * v, v * w, w * w)):
        total = jnp.where(lane == i, jnp.sum(product, axis=1, keepdims=True), total)
    sums[...] = jnp.broadcast_to(total, sums.shape)


def finish_kernel(ridge, parts, points, image, image_two, solution_out, residual_out, relative_out):
    total = jnp.sum(parts[...], axis=0, keepdims=True)
    bb, bv, vv, vw, ww = (total[:, i : i + 1] for i in range(5))
    rho = ridge[0]
    b_image = bv + rho * bb
    one = bb / b_image
    keep = 1.0 - one * rho
    mid = keep * keep * bb - 2.0 * keep * one * bv + one * one * vv
    curve = keep * keep * bv - 2.0 * keep * one * vv + one * one * vw
    ratio = mid / bb
    two = mid / (curve + rho * mid - ratio * mid / one)
    side = keep + ratio
    on_b = keep - two * rho * side
    on_v = -one - two * (side - rho * one)
    on_w = two * one
    b, v, w = points[5:6], image[...], image_two[...]
    solution_out[...] = (one + two * side) * b - (two * one) * v
    residual_out[...] = on_b * b + on_v * v + on_w * w
    end = (
        on_b * on_b * bb
        + 2.0 * on_b * on_v * bv
        + (on_v * on_v + 2.0 * on_b * on_w) * vv
        + 2.0 * on_v * on_w * vw
        + on_w * on_w * ww
    )
    relative_out[...] = jnp.broadcast_to(end / bb, relative_out.shape)


def call(kernel, outs, args, scalars=(), scratch=(), mib=20, flops=0):
    vmem = pl.BlockSpec(memory_space=pltpu.VMEM)
    smem = pl.BlockSpec(memory_space=pltpu.SMEM)
    shapes = tuple(jax.ShapeDtypeStruct(shape, dtype) for shape, dtype in outs)
    return pl.pallas_call(
        kernel,
        out_shape=shapes,
        in_specs=[smem if i in scalars else vmem for i in range(len(args))],
        out_specs=tuple(vmem for _ in outs),
        scratch_shapes=list(scratch),
        compiler_params=pltpu.CompilerParams(vmem_limit_bytes=mib << 20),
        cost_estimate=pl.CostEstimate(flops=flops, bytes_accessed=1 << 20, transcendentals=0),
    )(*args)


def solution(mesh):
    gx, gy = mesh.axis_names

    def pairs(axis):
        count = mesh.shape[axis]
        near = [(i, i ^ 1) for i in range(count)]
        far = [(i, (i + 1) % count if i % 2 else (i - 1) % count) for i in range(count)]
        return far, near

    def swap(axis, far, near):
        far_to, near_to = pairs(axis)
        return lax.ppermute(far, axis, far_to), lax.ppermute(near, axis, near_to)

    def shards(row_cells, col_cells, fracs, counts, targets, amplitude, lengthscale, ridge):
        n = targets.shape[2]
        spot = jnp.stack([lax.axis_index(gx) % 2, lax.axis_index(gy) % 2]).astype(jnp.int32)
        vector = ((1, n), f32)
        block = ((T, T), f32)
        main, edge = ((E, T), f32), ((8, 384), f32)
        slab, first_slab = ((SLAB, T), f32), ((SLAB + 16, T), f32)
        strip, corner = ((8, T), f32), ((8, 128), f32)
        row = ((T, 384), f32)
        scales = (main, ((E, 128), f32))
        scratch = (pltpu.VMEM((E, T), f32), pltpu.VMEM((8, 384), f32))

        ends = jnp.concatenate([amplitude[:8], amplitude[T - 8 :]], 0)
        live = (jnp.arange(n) < counts[0, 0]).astype(f32)
        cells = [row_cells[0, 0].astype(f32), col_cells[0, 0].astype(f32)]
        known = [fracs[0, 0, 0], fracs[1, 0, 0], live, targets[0, 0] * live]
        points = jnp.stack(cells + known + [jnp.zeros_like(live)] * 2)
        far_end, near_end = swap(gy, ends, ends)
        bands = call(bands_kernel, (((E, K), bf16),) * 4, (spot, lengthscale), (0, 1))
        x_bands, y_bands = bands[:2], bands[2:]
        half, twice = ((T, n), bf16), ((16, n), bf16)
        inner, rim = call(
            spread_kernel,
            (main, edge),
            (points,),
            flops=6 << 28,
        )
        inner, rim, turned, ends, far, near = call(
            first_slabs_kernel,
            (main, edge, block, strip, first_slab, first_slab),
            (spot, inner, rim, amplitude, far_end, near_end),
            (0,),
        )
        far, near = swap(gx, far, near)
        *across, far, near, outside, ends_corner, scale, scale_tail = call(
            first_across_kernel,
            (row, edge, strip, slab, slab, strip, corner, *scales),
            (spot, inner, rim, amplitude, turned, ends, far, near, *x_bands),
            (0,),
        )
        matrices = call(
            weights_kernel,
            (half, half, twice, ((E, n), f32), half, half, twice),
            (points, ends_corner),
            flops=3 << 28,
        )
        far, near = swap(gy, far, near)
        image, inner, rim, far, near = call(
            middle_kernel,
            (vector, main, edge, slab, slab),
            (
                spot, *across, far, near, *y_bands, scale, scale_tail, points,
                *matrices, turned, ends,
            ),
            (0,),
            scratch,
        )
        far, near = swap(gx, far, near)
        *across, far, near = call(
            across_kernel,
            (row, edge, strip, slab, slab),
            (spot, inner, rim, turned, ends, outside, ends_corner, far, near, *x_bands),
            (0,),
        )
        far, near = swap(gy, far, near)
        devices = mesh.size
        image_two, sums = call(
            last_kernel,
            (vector, ((devices, 128), f32)),
            (*across, far, near, *y_bands, scale, scale_tail, *matrices[3:], points, image),
            (),
        )
        parts = lax.all_to_all(sums.reshape(devices, 1, 128), (gx, gy), 0, 0)
        out, residual, relative = call(
            finish_kernel,
            (vector, vector, ((1, 128), f32)),
            (ridge, parts.reshape(devices, 128), points, image, image_two),
            (0,),
        )
        return out.reshape(1, 1, n), residual.reshape(1, 1, n), relative[0, :1]

    tiles = P(gy, gx, None)
    return jax.shard_map(
        shards,
        mesh=mesh,
        in_specs=(tiles, tiles, P(None, gy, gx, None), P(gy, gx), tiles, P(gy, gx), P(), P()),
        out_specs=(tiles, tiles, P()),
        check_vma=False,
    )
```

time: 103 us -> 90.8 us (0.88)
  waiting for transfers between devices: 35.6 us -> 24.5 us
  starting transfers between devices: 37.2 us -> 34.9 us
  other arithmetic: 0.15 us -> 1.6 us
    ppermute x10, waiting for transfers between devices: 23 us -> 12 us  [swap(): return (lax.ppermute(far, axis, far_to), lax.ppermute(near, axis, near_to))]
    all_to_all x1, starting transfers between devices: 12 us -> 10.5 us  [shards(): parts = lax.all_to_all(sums.reshape(devices, 1, 128), (gx, gy), 0, 0)]
    pallas_call x8 -> x9, Pallas kernels: 26 us -> 25.3 us  [call(): pl.pallas_call(kernel, out_shape=shapes, in_specs=[smem if i in scalars e...]
  transfers between devices with their start and end apart: 11 -> 11, of which waited for: 6 -> 6; matrix products, arithmetic and copies ran while one was open for 0% -> 3% of each run, Pallas kernels for 6% -> 10%
where the time goes in v1:
time: 90.8 us; the launch traced here: 90.1 us
  starting transfers between devices  34.9 us (38%)
  Pallas kernels  25.3 us (28%)
  waiting for transfers between devices  24.5 us (27%)
  between operations  2.06 us (2%)
  local copies, waits for them, and re-layouts  1.66 us (2%)
  other arithmetic  1.6 us (2%)
    pallas_call x9, Pallas kernels, call(): pl.pallas_call(kernel, out_shape=shapes, in_specs=[smem if i in scalars e...  25.3 us
    ppermute x10, starting transfers between devices, swap(): return (lax.ppermute(far, axis, far_to), lax.ppermute(near, axis, near_to))  24.4 us
    all_to_all x1, waiting for transfers between devices, shards(): parts = lax.all_to_all(sums.reshape(devices, 1, 128), (gx, gy), 0, 0)  12.6 us
    ppermute x10, waiting for transfers between devices, swap(): return (lax.ppermute(far, axis, far_to), lax.ppermute(near, axis, near_to))  12 us
    all_to_all x1, starting transfers between devices, shards(): parts = lax.all_to_all(sums.reshape(devices, 1, 128), (gx, gy), 0, 0)  10.5 us
  transfers between devices with their start and end apart: 11, of which 6 were waited for; matrix products, arithmetic and copies ran while one was open for 3% of the time, Pallas kernels for 10%

profile of v1, /device:TPU:1, one launch (start us, length us, event | category | flops | bytes accessed | tf_op | source)
XLA Modules:
  0.0 90.1 jit_solution(2843023301860973391)
XLA Ops:
  0.6 0.7 fusion
  1.4 4.3 %collective-permute-start = (f32[16,256]{1,0:T(8,128)S(1)}, f32[16,256]{1,0:T(8,128)S(1)}, u32[]{:S(2)}, u32[]{:S(2)}) collective-permute-start(f32[16,256]{1,0:T(8,128)S(1)} %pad_maximum_fusion), channel_id=1, source_target_pairs={{0,7},{1,2},{2,1},{3,4},{4,3},{5,6},{6,5},{7,0},{8,15},{9,10},{10,... | collective-permute-start | bytes 49160 | tf_op jit(solution)/shard_map/ppermute | solution.py:457
  5.7 0.0 collective-permute-start.1
  5.7 0.7 slice_bitcast_fusion
  7.1 0.8 convert_bitcast_fusion
  7.8 0.7 compare_select_fusion
  8.6 0.2 stack.23.points
  8.8 0.0 copy-start
  8.8 0.0 copy-start.1
  8.8 3.7 %shard_map.103 = (f32[264,256]{1,0:T(8,128)S(1)}, f32[8,384]{1,0:T(8,128)S(1)}) custom-call(f32[8,4096]{1,0:T(8,128)S(1)} %stack.23.points), custom_call_target="tpu_custom_call" | custom-call | flops 1610612736 | bytes 1048576 | tf_op jit(solution)/shard_map/pallas_call | solution.py:435
  12.6 0.1 pad_add_fusion.spot
  12.6 0.0 collective-permute-done.far_ends
  12.6 0.0 collective-permute-done.1.near_ends
  12.6 0.0 copy-done
  12.6 0.7 shard_map.104
  13.4 3.5 %collective-permute-start.2 = (f32[160,256]{1,0:T(8,128)S(1)}, f32[160,256]{1,0:T(8,128)S(1)}, u32[]{:S(2)}, u32[]{:S(2)}) collective-permute-start(f32[160,256]{1,0:T(8,128)S(1)} %get-tuple-element.52), channel_id=1, source_target_pairs={{0,248},{8,16},{16,8},{24,32},{32,24},{40,48},{48,40},{56,64},{64,... | collective-permute-start | bytes 491528 | tf_op jit(solution)/shard_map/ppermute | solution.py:457
  16.9 4.8 %collective-permute-start.3 = (f32[160,256]{1,0:T(8,128)S(1)}, f32[160,256]{1,0:T(8,128)S(1)}, u32[]{:S(2)}, u32[]{:S(2)}) collective-permute-start(f32[160,256]{1,0:T(8,128)S(1)} %get-tuple-element.53), channel_id=1, source_target_pairs={{0,8},{8,0},{16,24},{24,16},{32,40},{40,32},{48,56},{56,48},{64,72... | collective-permute-start | bytes 491528 | tf_op jit(solution)/shard_map/ppermute | solution.py:457
  21.8 0.0 copy-done.1
  21.8 1.2 %shard_map.105 = (bf16[264,640]{1,0:T(8,128)(2,1)S(1)}, bf16[264,640]{1,0:T(8,128)(2,1)S(1)}, bf16[264,640]{1,0:T(8,128)(2,1)S(1)}, bf16[264,640]{1,0:T(8,128)(2,1)S(1)}) custom-call(s32[2]{0:T(128)S(1)} %pad_add_fusion.spot, f32[2]{0:T(128)S(1)} %copy-done.1), custom_call_target="tpu_custom_call" | custom-call | bytes 1048576 | tf_op jit(solution)/shard_map/pallas_call | solution.py:435
  22.9 0.0 collective-permute-done.2.far
  22.9 0.0 collective-permute-done.3.near
  23.0 1.3 %shard_map.106 = (f32[256,384]{1,0:T(8,128)S(1)}, f32[8,384]{1,0:T(8,128)S(1)}, f32[8,256]{1,0:T(8,128)S(1)}, f32[144,256]{1,0:T(8,128)S(1)}, f32[144,256]{1,0:T...) custom-call(s32[2]{0:T(128)S(1)} %pad_add_fusion.spot, ...), custom_call_target="tpu_custom_call" | custom-call | bytes 1048576 | tf_op jit(solution)/shard_map/pallas_call | solution.py:435
  24.3 1.2 %collective-permute-start.4 = (f32[144,256]{1,0:T(8,128)S(1)}, f32[144,256]{1,0:T(8,128)S(1)}, u32[]{:S(2)}, u32[]{:S(2)}) collective-permute-start(f32[144,256]{1,0:T(8,128)S(1)} %get-tuple-element.59), channel_id=1, source_target_pairs={{0,7},{1,2},{2,1},{3,4},{4,3},{5,6},{6,5},{7,0},{8,15},{9,10},{10,... | collective-permute-start | bytes 442376 | tf_op jit(solution)/shard_map/ppermute | solution.py:457
  25.5 0.5 collective-permute-start.5
  26.0 4.5 %shard_map.107 = (bf16[256,4096]{1,0:T(8,128)(2,1)S(1)}, bf16[256,4096]{1,0:T(8,128)(2,1)S(1)}, bf16[16,4096]{1,0:T(8,128)(2,1)S(1)}, f32[264,4096]{1,0:T(8,128)...) custom-call(f32[8,4096]{1,0:T(8,128)S(1)} %stack.23.points, ...), custom_call_target="tpu_custom_call" | custom-call | flops 805306368 | bytes 1048576 | tf_op jit(solution)/shard_map/pallas_call | solution.py:435
  30.5 0.1 collective-permute-done.4.far
  30.6 2.9 %collective-permute-done.5.near = f32[144,256]{1,0:T(8,128)S(1)} collective-permute-done((f32[144,256]{1,0:T(8,128)S(1)}, f32[144,256]{1,0:T(8,128)S(1)}, u32[]{:S(2)}, u32[]{:S(2)}) %collective-permute-start.5) | collective-permute-done | bytes 147488 | tf_op jit(solution)/shard_map/ppermute | solution.py:457
  33.5 7.6 %shard_map.108 = (f32[1,4096]{1,0:T(1,128)S(1)}, f32[264,256]{1,0:T(8,128)S(1)}, f32[8,384]{1,0:T(8,128)S(1)}, f32[144,256]{1,0:T(8,128)S(1)}, f32[144,256]{1,0:T(8,128)S(1)}) custom-call(s32[2]{0:T(128)S(1)} %pad_add_fusion.spot, f32[256,384]{1,0:T(8,128)S(1)} %get-tuple-element.56.row, f32[8,384]{1,0:T(8,128)S(1)} %get-tuple-element.57.group, ...), custom_call_target="tpu_custom_call" | custom-call | bytes 1048576 | tf_op jit(solution)/shard_map/pallas_call | solution.py:435
  41.1 2.4 %collective-permute-start.6 = (f32[144,256]{1,0:T(8,128)S(1)}, f32[144,256]{1,0:T(8,128)S(1)}, u32[]{:S(2)}, u32[]{:S(2)}) collective-permute-start(f32[144,256]{1,0:T(8,128)S(1)} %get-tuple-element.76), channel_id=1, source_target_pairs={{0,248},{8,16},{16,8},{24,32},{32,24},{40,48},{48,40},{56,64},{64,... | collective-permute-start | bytes 442376 | tf_op jit(solution)/shard_map/ppermute | solution.py:457
  43.5 6.1 %collective-permute-start.7 = (f32[144,256]{1,0:T(8,128)S(1)}, f32[144,256]{1,0:T(8,128)S(1)}, u32[]{:S(2)}, u32[]{:S(2)}) collective-permute-start(f32[144,256]{1,0:T(8,128)S(1)} %get-tuple-element.77), channel_id=1, source_target_pairs={{0,8},{8,0},{16,24},{24,16},{32,40},{40,32},{48,56},{56,48},{64,72... | collective-permute-start | bytes 442376 | tf_op jit(solution)/shard_map/ppermute | solution.py:457
  49.6 0.0 collective-permute-done.6.far
  49.6 1.0 %collective-permute-done.7.near = f32[144,256]{1,0:T(8,128)S(1)} collective-permute-done((f32[144,256]{1,0:T(8,128)S(1)}, f32[144,256]{1,0:T(8,128)S(1)}, u32[]{:S(2)}, u32[]{:S(2)}) %collective-permute-start.7) | collective-permute-done | bytes 147488 | tf_op jit(solution)/shard_map/ppermute | solution.py:457
  50.6 1.4 %shard_map.109 = (f32[256,384]{1,0:T(8,128)S(1)}, f32[8,384]{1,0:T(8,128)S(1)}, f32[8,256]{1,0:T(8,128)S(1)}, f32[144,256]{1,0:T(8,128)S(1)}, f32[144,256]{1,0:T(8,128)S(1)}) custom-call(s32[2]{0:T(128)S(1)} %pad_add_fusion.spot, f32[264,256]{1,0:T(8,128)S(1)} %get-tuple-element.73.main, f32[8,384]{1,0:T(8,128)S(1)} %get-tuple-element.74.edge, ...), custom_call_target="tpu_custom_call" | custom-call | bytes 1048576 | tf_op jit(solution)/shard_map/pallas_call | solution.py:435
  51.9 1.5 %collective-permute-start.8 = (f32[144,256]{1,0:T(8,128)S(1)}, f32[144,256]{1,0:T(8,128)S(1)}, u32[]{:S(2)}, u32[]{:S(2)}) collective-permute-start(f32[144,256]{1,0:T(8,128)S(1)} %get-tuple-element.81), channel_id=1, source_target_pairs={{0,7},{1,2},{2,1},{3,4},{4,3},{5,6},{6,5},{7,0},{8,15},{9,10},{10,... | collective-permute-start | bytes 442376 | tf_op jit(solution)/shard_map/ppermute | solution.py:457
  53.5 0.0 collective-permute-start.9
  53.5 5.0 %collective-permute-done.8.far = f32[144,256]{1,0:T(8,128)S(1)} collective-permute-done((f32[144,256]{1,0:T(8,128)S(1)}, f32[144,256]{1,0:T(8,128)S(1)}, u32[]{:S(2)}, u32[]{:S(2)}) %collective-permute-start.8) | collective-permute-done | bytes 147488 | tf_op jit(solution)/shard_map/ppermute | solution.py:457
  58.5 3.0 %collective-permute-done.9.near = f32[144,256]{1,0:T(8,128)S(1)} collective-permute-done((f32[144,256]{1,0:T(8,128)S(1)}, f32[144,256]{1,0:T(8,128)S(1)}, u32[]{:S(2)}, u32[]{:S(2)}) %collective-permute-start.9) | collective-permute-done | bytes 147488 | tf_op jit(solution)/shard_map/ppermute | solution.py:457
  61.5 3.9 %shard_map.110 = (f32[1,4096]{1,0:T(1,128)S(1)}, f32[256,128]{1,0:T(8,128)}) custom-call(f32[256,384]{1,0:T(8,128)S(1)} %get-tuple-element.78.row, f32[8,384]{1,0:T(8,128)S(1)} %get-tuple-element.79.group, f32[8,256]{1,0:T(8,128)S(1)} %get-tuple-element.80.tail, f32[144,256]{1,0:T(8,128)S(1)} %collective-permute-done.8.far, ...), custom_call_target="tpu_custom_call" | custom-call | bytes 1048576 | tf_op jit(solution)/shard_map/pallas_call | solution.py:435
  65.4 10.5 %all-to-all-start = ((f32[256,1,128]{2,1,0:T(1,128)}), f32[256,1,128]{2,1,0:T(1,128)S(1)}, u32[]{:S(2)}, u32[]{:S(2)}) async-start(f32[256,1,128]{2,1,0:T(1,128)} %bitcast.9), calls=%async_computation | async-start | bytes 262144 | tf_op jit(solution)/shard_map/all_to_all | solution.py:531
  76.6 12.6 %all-to-all-done = f32[256,1,128]{2,1,0:T(1,128)S(1)} async-done(((f32[256,1,128]{2,1,0:T(1,128)}), f32[256,1,128]{2,1,0:T(1,128)S(1)}, u32[]{:S(2)}, u32[]{:S(2)}) %all-to-all-start) | async-done | bytes 131104 | tf_op jit(solution)/shard_map/all_to_all | solution.py:531
  89.1 0.9 %shard_map.111 = (f32[1,4096]{1,0:T(1,128)}, f32[1,4096]{1,0:T(1,128)}, f32[1,128]{1,0:T(1,128)}) custom-call(f32[1]{0:T(128)S(6)} %copy.13.ridge, f32[256,128]{1,0:T(8,128)S(1)} %bitcast.23, f32[8,4096]{1,0:T(8,128)S(1)} %stack.23.points, f32[1,4096]{1,0:T(1,128)S(1)} %get-tuple-element.83.image, f32[1,4096]{1,0:T(1,128)S(1)} %get-tuple-element.85.image_two), custom_call_target="tpu_custom_call" | custom-call | bytes 1048576 | tf_op jit(solution)/shard_map/pallas_call | solution.py:435
  (3 shorter events, 0.0 us)
Async XLA Ops:
  1.4 11.3 %collective-permute-start = (f32[16,256]{1,0:T(8,128)S(1)}, f32[16,256]{1,0:T(8,128)S(1)}, u32[]{:S(2)}, u32[]{:S(2)}) collective-permute-start(f32[16,256]{1,0:T(8,128)S(1)} %pad_maximum_fusion), channel_id=1, source_target_pairs={{0,7},{1,2},{2,1},{3,4},{4,3},{5,6},{6,5},{7,0},{8,15},{9,10},{10,... | collective-permute-start | bytes 49160 | tf_op jit(solution)/shard_map/ppermute | solution.py:457
  5.7 7.0 %collective-permute-start.1 = (f32[16,256]{1,0:T(8,128)S(1)}, f32[16,256]{1,0:T(8,128)S(1)}, u32[]{:S(2)}, u32[]{:S(2)}) collective-permute-start(f32[16,256]{1,0:T(8,128)S(1)} %pad_maximum_fusion), channel_id=1, source_target_pairs={{0,1},{1,0},{2,3},{3,2},{4,5},{5,4},{6,7},{7,6},{8,9},{9,8},{10,11... | collective-permute-start | bytes 49160 | tf_op jit(solution)/shard_map/ppermute | solution.py:457
  8.8 3.8 %copy-start = (f32[256,256]{1,0:T(8,128)S(1)}, f32[256,256]{1,0:T(8,128)}, u32[]{:S(2)}) copy-start(f32[256,256]{1,0:T(8,128)} %amplitude.3) | copy-start | bytes 786436
  8.8 13.0 %copy-start.1 = (f32[2]{0:T(128)S(1)}, f32[2]{0:T(128)}, u32[]{:S(2)}) copy-start(f32[2]{0:T(128)} %scales.1) | copy-start | bytes 28
  13.4 9.6 %collective-permute-start.2 = (f32[160,256]{1,0:T(8,128)S(1)}, f32[160,256]{1,0:T(8,128)S(1)}, u32[]{:S(2)}, u32[]{:S(2)}) collective-permute-start(f32[160,256]{1,0:T(8,128)S(1)} %get-tuple-element.52), channel_id=1, source_target_pairs={{0,248},{8,16},{16,8},{24,32},{32,24},{40,48},{48,40},{56,64},{64,... | collective-permute-start | bytes 491528 | tf_op jit(solution)/shard_map/ppermute | solution.py:457
  16.9 6.0 %collective-permute-start.3 = (f32[160,256]{1,0:T(8,128)S(1)}, f32[160,256]{1,0:T(8,128)S(1)}, u32[]{:S(2)}, u32[]{:S(2)}) collective-permute-start(f32[160,256]{1,0:T(8,128)S(1)} %get-tuple-element.53), channel_id=1, source_target_pairs={{0,8},{8,0},{16,24},{24,16},{32,40},{40,32},{48,56},{56,48},{64,72... | collective-permute-start | bytes 491528 | tf_op jit(solution)/shard_map/ppermute | solution.py:457
  24.3 6.3 %collective-permute-start.4 = (f32[144,256]{1,0:T(8,128)S(1)}, f32[144,256]{1,0:T(8,128)S(1)}, u32[]{:S(2)}, u32[]{:S(2)}) collective-permute-start(f32[144,256]{1,0:T(8,128)S(1)} %get-tuple-element.59), channel_id=1, source_target_pairs={{0,7},{1,2},{2,1},{3,4},{4,3},{5,6},{6,5},{7,0},{8,15},{9,10},{10,... | collective-permute-start | bytes 442376 | tf_op jit(solution)/shard_map/ppermute | solution.py:457
  25.5 7.9 %collective-permute-start.5 = (f32[144,256]{1,0:T(8,128)S(1)}, f32[144,256]{1,0:T(8,128)S(1)}, u32[]{:S(2)}, u32[]{:S(2)}) collective-permute-start(f32[144,256]{1,0:T(8,128)S(1)} %get-tuple-element.60), channel_id=1, source_target_pairs={{0,1},{1,0},{2,3},{3,2},{4,5},{5,4},{6,7},{7,6},{8,9},{9,8},{10,11... | collective-permute-start | bytes 442376 | tf_op jit(solution)/shard_map/ppermute | solution.py:457
  41.1 8.5 %collective-permute-start.6 = (f32[144,256]{1,0:T(8,128)S(1)}, f32[144,256]{1,0:T(8,128)S(1)}, u32[]{:S(2)}, u32[]{:S(2)}) collective-permute-start(f32[144,256]{1,0:T(8,128)S(1)} %get-tuple-element.76), channel_id=1, source_target_pairs={{0,248},{8,16},{16,8},{24,32},{32,24},{40,48},{48,40},{56,64},{64,... | collective-permute-start | bytes 442376 | tf_op jit(solution)/shard_map/ppermute | solution.py:457
  43.5 7.1 %collective-permute-start.7 = (f32[144,256]{1,0:T(8,128)S(1)}, f32[144,256]{1,0:T(8,128)S(1)}, u32[]{:S(2)}, u32[]{:S(2)}) collective-permute-start(f32[144,256]{1,0:T(8,128)S(1)} %get-tuple-element.77), channel_id=1, source_target_pairs={{0,8},{8,0},{16,24},{24,16},{32,40},{40,32},{48,56},{56,48},{64,72... | collective-permute-start | bytes 442376 | tf_op jit(solution)/shard_map/ppermute | solution.py:457
  51.9 6.5 %collective-permute-start.8 = (f32[144,256]{1,0:T(8,128)S(1)}, f32[144,256]{1,0:T(8,128)S(1)}, u32[]{:S(2)}, u32[]{:S(2)}) collective-permute-start(f32[144,256]{1,0:T(8,128)S(1)} %get-tuple-element.81), channel_id=1, source_target_pairs={{0,7},{1,2},{2,1},{3,4},{4,3},{5,6},{6,5},{7,0},{8,15},{9,10},{10,... | collective-permute-start | bytes 442376 | tf_op jit(solution)/shard_map/ppermute | solution.py:457
  53.5 8.0 %collective-permute-start.9 = (f32[144,256]{1,0:T(8,128)S(1)}, f32[144,256]{1,0:T(8,128)S(1)}, u32[]{:S(2)}, u32[]{:S(2)}) collective-permute-start(f32[144,256]{1,0:T(8,128)S(1)} %get-tuple-element.82), channel_id=1, source_target_pairs={{0,1},{1,0},{2,3},{3,2},{4,5},{5,4},{6,7},{7,6},{8,9},{9,8},{10,11... | collective-permute-start | bytes 442376 | tf_op jit(solution)/shard_map/ppermute | solution.py:457
  65.4 23.7 %all-to-all-start = ((f32[256,1,128]{2,1,0:T(1,128)}), f32[256,1,128]{2,1,0:T(1,128)S(1)}, u32[]{:S(2)}, u32[]{:S(2)}) async-start(f32[256,1,128]{2,1,0:T(1,128)} %bitcast.9), calls=%async_computation | async-start | bytes 262144 | tf_op jit(solution)/shard_map/all_to_all | solution.py:531

commit v2 on v1

--- a/solution.py
+++ b/solution.py
@@ -106,11 +106,14 @@
 
 
 def pick(grid, c_main, c_pair, r):
-    high, low, tail = grid
-    pack = jnp.concatenate([c_pair, c_pair], 0)
+    high, low, tails = grid
     value = dot(high, c_main[0], MM) + dot(high, c_main[1], MM) + dot(low, c_main[0], MM)
-    value = value + dot(tail, pack, MM)
-    return jnp.sum(value * r, axis=0, keepdims=True)
+    out = jnp.sum(value * r, axis=0, keepdims=True)
+    c_tail = c_pair.astype(f32)
+    for i, tail in enumerate(tails):
+        across = jnp.sum(jnp.concatenate([tail] * (STEP // 128), 1) * r, axis=0, keepdims=True)
+        out = out + across * (c_tail[i : i + 1] + c_tail[8 + i : 9 + i])
+    return out
 
 
 def put(row, value, index, x):
@@ -335,10 +338,7 @@
     side = side + smooth_by((yh[:, 2 * T : FIELD], yl[:, 2 * T : FIELD]), ends)[:, :8]
     side = side * scale_tail[:, :8]
     high, low = split(main)
-    side_high = side.astype(bf16).astype(f32)
-    side_low = side - side_high
-    zero = jnp.zeros_like(side)
-    return high, low, jnp.concatenate([side_high, side_high, side_low, zero], 1).astype(bf16)
+    return high, low, [jnp.broadcast_to(side[:, i : i + 1], (E, 128)) for i in range(3)]
 
 
 def stencil(cells, fraction, live):
@@ -454,7 +454,9 @@
 
     def swap(axis, far, near):
         far_to, near_to = pairs(axis)
-        return lax.ppermute(far, axis, far_to), lax.ppermute(near, axis, near_to)
+        near = lax.ppermute(near, axis, near_to)
+        far = lax.ppermute(far, axis, far_to)
+        return far, near
 
     def shards(row_cells, col_cells, fracs, counts, targets, amplitude, lengthscale, ridge):
         n = targets.shape[2]

time: 90.8 us -> 90.3 us (level)
  transfers between devices with their start and end apart: 11 -> 11, of which waited for: 6 -> 6; matrix products, arithmetic and copies ran while one was open for 3% -> 3% of each run, Pallas kernels for 10% -> 11%
where the time goes in v2:
time: 90.3 us; the launch traced here: 89.5 us
  starting transfers between devices  34.9 us (39%)
  Pallas kernels  24.7 us (27%)
  waiting for transfers between devices  24.5 us (27%)
  between operations  2.06 us (2%)
  local copies, waits for them, and re-layouts  1.66 us (2%)
  other arithmetic  1.6 us (2%)
    pallas_call x9, Pallas kernels, call(): pl.pallas_call(kernel, out_shape=shapes, in_specs=[smem if i in scalars e...  24.7 us
    ppermute x5, starting transfers between devices, swap(): far = lax.ppermute(far, axis, far_to)  13 us
    all_to_all x1, waiting for transfers between devices, shards(): parts = lax.all_to_all(sums.reshape(devices, 1, 128), (gx, gy), 0, 0)  12.6 us
    ppermute x5, starting transfers between devices, swap(): near = lax.ppermute(near, axis, near_to)  11.4 us
    all_to_all x1, starting transfers between devices, shards(): parts = lax.all_to_all(sums.reshape(devices, 1, 128), (gx, gy), 0, 0)  10.5 us
    ppermute x5, waiting for transfers between devices, swap(): near = lax.ppermute(near, axis, near_to)  6.88 us
    ppermute x5, waiting for transfers between devices, swap(): far = lax.ppermute(far, axis, far_to)  5.12 us
  transfers between devices with their start and end apart: 11, of which 6 were waited for; matrix products, arithmetic and copies ran while one was open for 3% of the time, Pallas kernels for 11%

profile of v2, /device:TPU:1, one launch (start us, length us, event | category | flops | bytes accessed | tf_op | source)
XLA Modules:
  0.0 89.5 jit_solution(11896053558250966460)
XLA Ops:
  0.6 0.7 fusion
  1.4 4.3 %collective-permute-start = (f32[16,256]{1,0:T(8,128)S(1)}, f32[16,256]{1,0:T(8,128)S(1)}, u32[]{:S(2)}, u32[]{:S(2)}) collective-permute-start(f32[16,256]{1,0:T(8,128)S(1)} %pad_maximum_fusion), channel_id=1, source_target_pairs={{0,7},{1,2},{2,1},{3,4},{4,3},{5,6},{6,5},{7,0},{8,15},{9,10},{10,... | collective-permute-start | bytes 49160 | tf_op jit(solution)/shard_map/ppermute | solution.py:458
  5.7 0.0 collective-permute-start.1
  5.7 0.7 slice_bitcast_fusion
  7.1 0.8 convert_bitcast_fusion
  7.8 0.7 compare_select_fusion
  8.6 0.2 stack.23.points
  8.8 0.0 copy-start
  8.8 0.0 copy-start.1
  8.8 3.7 %shard_map.103 = (f32[264,256]{1,0:T(8,128)S(1)}, f32[8,384]{1,0:T(8,128)S(1)}) custom-call(f32[8,4096]{1,0:T(8,128)S(1)} %stack.23.points), custom_call_target="tpu_custom_call" | custom-call | flops 1610612736 | bytes 1048576 | tf_op jit(solution)/shard_map/pallas_call | solution.py:435
  12.6 0.1 pad_add_fusion.spot
  12.6 0.0 collective-permute-done.far_ends
  12.6 0.0 collective-permute-done.1.near_ends
  12.6 0.0 copy-done
  12.6 0.7 shard_map.104
  13.4 3.5 %collective-permute-start.2 = (f32[160,256]{1,0:T(8,128)S(1)}, f32[160,256]{1,0:T(8,128)S(1)}, u32[]{:S(2)}, u32[]{:S(2)}) collective-permute-start(f32[160,256]{1,0:T(8,128)S(1)} %get-tuple-element.52), channel_id=1, source_target_pairs={{0,248},{8,16},{16,8},{24,32},{32,24},{40,48},{48,40},{56,64},{64,... | collective-permute-start | bytes 491528 | tf_op jit(solution)/shard_map/ppermute | solution.py:458
  16.9 4.8 %collective-permute-start.3 = (f32[160,256]{1,0:T(8,128)S(1)}, f32[160,256]{1,0:T(8,128)S(1)}, u32[]{:S(2)}, u32[]{:S(2)}) collective-permute-start(f32[160,256]{1,0:T(8,128)S(1)} %get-tuple-element.53), channel_id=1, source_target_pairs={{0,8},{8,0},{16,24},{24,16},{32,40},{40,32},{48,56},{56,48},{64,72... | collective-permute-start | bytes 491528 | tf_op jit(solution)/shard_map/ppermute | solution.py:457
  21.8 0.0 copy-done.1
  21.8 1.2 %shard_map.105 = (bf16[264,640]{1,0:T(8,128)(2,1)S(1)}, bf16[264,640]{1,0:T(8,128)(2,1)S(1)}, bf16[264,640]{1,0:T(8,128)(2,1)S(1)}, bf16[264,640]{1,0:T(8,128)(2,1)S(1)}) custom-call(s32[2]{0:T(128)S(1)} %pad_add_fusion.spot, f32[2]{0:T(128)S(1)} %copy-done.1), custom_call_target="tpu_custom_call" | custom-call | bytes 1048576 | tf_op jit(solution)/shard_map/pallas_call | solution.py:435
  22.9 0.0 collective-permute-done.2.far
  22.9 0.0 collective-permute-done.3.near
  23.0 1.3 %shard_map.106 = (f32[256,384]{1,0:T(8,128)S(1)}, f32[8,384]{1,0:T(8,128)S(1)}, f32[8,256]{1,0:T(8,128)S(1)}, f32[144,256]{1,0:T(8,128)S(1)}, f32[144,256]{1,0:T...) custom-call(s32[2]{0:T(128)S(1)} %pad_add_fusion.spot, ...), custom_call_target="tpu_custom_call" | custom-call | bytes 1048576 | tf_op jit(solution)/shard_map/pallas_call | solution.py:435
  24.3 1.2 %collective-permute-start.4 = (f32[144,256]{1,0:T(8,128)S(1)}, f32[144,256]{1,0:T(8,128)S(1)}, u32[]{:S(2)}, u32[]{:S(2)}) collective-permute-start(f32[144,256]{1,0:T(8,128)S(1)} %get-tuple-element.59), channel_id=1, source_target_pairs={{0,7},{1,2},{2,1},{3,4},{4,3},{5,6},{6,5},{7,0},{8,15},{9,10},{10,... | collective-permute-start | bytes 442376 | tf_op jit(solution)/shard_map/ppermute | solution.py:458
  25.5 0.5 collective-permute-start.5
  26.0 4.5 %shard_map.107 = (bf16[256,4096]{1,0:T(8,128)(2,1)S(1)}, bf16[256,4096]{1,0:T(8,128)(2,1)S(1)}, bf16[16,4096]{1,0:T(8,128)(2,1)S(1)}, f32[264,4096]{1,0:T(8,128)...) custom-call(f32[8,4096]{1,0:T(8,128)S(1)} %stack.23.points, ...), custom_call_target="tpu_custom_call" | custom-call | flops 805306368 | bytes 1048576 | tf_op jit(solution)/shard_map/pallas_call | solution.py:435
  30.5 0.1 collective-permute-done.4.far
  30.6 2.9 %collective-permute-done.5.near = f32[144,256]{1,0:T(8,128)S(1)} collective-permute-done((f32[144,256]{1,0:T(8,128)S(1)}, f32[144,256]{1,0:T(8,128)S(1)}, u32[]{:S(2)}, u32[]{:S(2)}) %collective-permute-start.5) | collective-permute-done | bytes 147488 | tf_op jit(solution)/shard_map/ppermute | solution.py:457
  33.5 7.4 %shard_map.108 = (f32[1,4096]{1,0:T(1,128)S(1)}, f32[264,256]{1,0:T(8,128)S(1)}, f32[8,384]{1,0:T(8,128)S(1)}, f32[144,256]{1,0:T(8,128)S(1)}, f32[144,256]{1,0:T(8,128)S(1)}) custom-call(s32[2]{0:T(128)S(1)} %pad_add_fusion.spot, f32[256,384]{1,0:T(8,128)S(1)} %get-tuple-element.56.row, f32[8,384]{1,0:T(8,128)S(1)} %get-tuple-element.57.group, ...), custom_call_target="tpu_custom_call" | custom-call | bytes 1048576 | tf_op jit(solution)/shard_map/pallas_call | solution.py:435
  40.9 2.4 %collective-permute-start.6 = (f32[144,256]{1,0:T(8,128)S(1)}, f32[144,256]{1,0:T(8,128)S(1)}, u32[]{:S(2)}, u32[]{:S(2)}) collective-permute-start(f32[144,256]{1,0:T(8,128)S(1)} %get-tuple-element.76), channel_id=1, source_target_pairs={{0,248},{8,16},{16,8},{24,32},{32,24},{40,48},{48,40},{56,64},{64,... | collective-permute-start | bytes 442376 | tf_op jit(solution)/shard_map/ppermute | solution.py:458
  43.3 6.1 %collective-permute-start.7 = (f32[144,256]{1,0:T(8,128)S(1)}, f32[144,256]{1,0:T(8,128)S(1)}, u32[]{:S(2)}, u32[]{:S(2)}) collective-permute-start(f32[144,256]{1,0:T(8,128)S(1)} %get-tuple-element.77), channel_id=1, source_target_pairs={{0,8},{8,0},{16,24},{24,16},{32,40},{40,32},{48,56},{56,48},{64,72... | collective-permute-start | bytes 442376 | tf_op jit(solution)/shard_map/ppermute | solution.py:457
  49.4 0.0 collective-permute-done.6.far
  49.4 1.0 %collective-permute-done.7.near = f32[144,256]{1,0:T(8,128)S(1)} collective-permute-done((f32[144,256]{1,0:T(8,128)S(1)}, f32[144,256]{1,0:T(8,128)S(1)}, u32[]{:S(2)}, u32[]{:S(2)}) %collective-permute-start.7) | collective-permute-done | bytes 147488 | tf_op jit(solution)/shard_map/ppermute | solution.py:457
  50.4 1.3 %shard_map.109 = (f32[256,384]{1,0:T(8,128)S(1)}, f32[8,384]{1,0:T(8,128)S(1)}, f32[8,256]{1,0:T(8,128)S(1)}, f32[144,256]{1,0:T(8,128)S(1)}, f32[144,256]{1,0:T(8,128)S(1)}) custom-call(s32[2]{0:T(128)S(1)} %pad_add_fusion.spot, f32[264,256]{1,0:T(8,128)S(1)} %get-tuple-element.73.main, f32[8,384]{1,0:T(8,128)S(1)} %get-tuple-element.74.edge, ...), custom_call_target="tpu_custom_call" | custom-call | bytes 1048576 | tf_op jit(solution)/shard_map/pallas_call | solution.py:435
  51.8 1.5 %collective-permute-start.8 = (f32[144,256]{1,0:T(8,128)S(1)}, f32[144,256]{1,0:T(8,128)S(1)}, u32[]{:S(2)}, u32[]{:S(2)}) collective-permute-start(f32[144,256]{1,0:T(8,128)S(1)} %get-tuple-element.81), channel_id=1, source_target_pairs={{0,7},{1,2},{2,1},{3,4},{4,3},{5,6},{6,5},{7,0},{8,15},{9,10},{10,... | collective-permute-start | bytes 442376 | tf_op jit(solution)/shard_map/ppermute | solution.py:458
  53.3 0.0 collective-permute-start.9
  53.3 5.0 %collective-permute-done.8.far = f32[144,256]{1,0:T(8,128)S(1)} collective-permute-done((f32[144,256]{1,0:T(8,128)S(1)}, f32[144,256]{1,0:T(8,128)S(1)}, u32[]{:S(2)}, u32[]{:S(2)}) %collective-permute-start.8) | collective-permute-done | bytes 147488 | tf_op jit(solution)/shard_map/ppermute | solution.py:458
  58.3 3.0 %collective-permute-done.9.near = f32[144,256]{1,0:T(8,128)S(1)} collective-permute-done((f32[144,256]{1,0:T(8,128)S(1)}, f32[144,256]{1,0:T(8,128)S(1)}, u32[]{:S(2)}, u32[]{:S(2)}) %collective-permute-start.9) | collective-permute-done | bytes 147488 | tf_op jit(solution)/shard_map/ppermute | solution.py:457
  61.3 3.6 %shard_map.110 = (f32[1,4096]{1,0:T(1,128)S(1)}, f32[256,128]{1,0:T(8,128)}) custom-call(f32[256,384]{1,0:T(8,128)S(1)} %get-tuple-element.78.row, f32[8,384]{1,0:T(8,128)S(1)} %get-tuple-element.79.group, f32[8,256]{1,0:T(8,128)S(1)} %get-tuple-element.80.tail, f32[144,256]{1,0:T(8,128)S(1)} %collective-permute-done.8.far, ...), custom_call_target="tpu_custom_call" | custom-call | bytes 1048576 | tf_op jit(solution)/shard_map/pallas_call | solution.py:435
  64.8 10.5 %all-to-all-start = ((f32[256,1,128]{2,1,0:T(1,128)}), f32[256,1,128]{2,1,0:T(1,128)S(1)}, u32[]{:S(2)}, u32[]{:S(2)}) async-start(f32[256,1,128]{2,1,0:T(1,128)} %bitcast.9), calls=%async_computation | async-start | bytes 262144 | tf_op jit(solution)/shard_map/all_to_all | solution.py:533
  76.0 12.6 %all-to-all-done = f32[256,1,128]{2,1,0:T(1,128)S(1)} async-done(((f32[256,1,128]{2,1,0:T(1,128)}), f32[256,1,128]{2,1,0:T(1,128)S(1)}, u32[]{:S(2)}, u32[]{:S(2)}) %all-to-all-start) | async-done | bytes 131104 | tf_op jit(solution)/shard_map/all_to_all | solution.py:533
  88.6 0.9 %shard_map.111 = (f32[1,4096]{1,0:T(1,128)}, f32[1,4096]{1,0:T(1,128)}, f32[1,128]{1,0:T(1,128)}) custom-call(f32[1]{0:T(128)S(6)} %copy.13.ridge, f32[256,128]{1,0:T(8,128)S(1)} %bitcast.23, f32[8,4096]{1,0:T(8,128)S(1)} %stack.23.points, f32[1,4096]{1,0:T(1,128)S(1)} %get-tuple-element.83.image, f32[1,4096]{1,0:T(1,128)S(1)} %get-tuple-element.85.image_two), custom_call_target="tpu_custom_call" | custom-call | bytes 1048576 | tf_op jit(solution)/shard_map/pallas_call | solution.py:435
  (3 shorter events, 0.0 us)
Async XLA Ops:
  1.4 11.3 %collective-permute-start = (f32[16,256]{1,0:T(8,128)S(1)}, f32[16,256]{1,0:T(8,128)S(1)}, u32[]{:S(2)}, u32[]{:S(2)}) collective-permute-start(f32[16,256]{1,0:T(8,128)S(1)} %pad_maximum_fusion), channel_id=1, source_target_pairs={{0,7},{1,2},{2,1},{3,4},{4,3},{5,6},{6,5},{7,0},{8,15},{9,10},{10,... | collective-permute-start | bytes 49160 | tf_op jit(solution)/shard_map/ppermute | solution.py:458
  5.7 7.0 %collective-permute-start.1 = (f32[16,256]{1,0:T(8,128)S(1)}, f32[16,256]{1,0:T(8,128)S(1)}, u32[]{:S(2)}, u32[]{:S(2)}) collective-permute-start(f32[16,256]{1,0:T(8,128)S(1)} %pad_maximum_fusion), channel_id=1, source_target_pairs={{0,1},{1,0},{2,3},{3,2},{4,5},{5,4},{6,7},{7,6},{8,9},{9,8},{10,11... | collective-permute-start | bytes 49160 | tf_op jit(solution)/shard_map/ppermute | solution.py:457
  8.8 3.8 %copy-start = (f32[256,256]{1,0:T(8,128)S(1)}, f32[256,256]{1,0:T(8,128)}, u32[]{:S(2)}) copy-start(f32[256,256]{1,0:T(8,128)} %amplitude.3) | copy-start | bytes 786436
  8.8 13.0 %copy-start.1 = (f32[2]{0:T(128)S(1)}, f32[2]{0:T(128)}, u32[]{:S(2)}) copy-start(f32[2]{0:T(128)} %scales.1) | copy-start | bytes 28
  13.4 9.6 %collective-permute-start.2 = (f32[160,256]{1,0:T(8,128)S(1)}, f32[160,256]{1,0:T(8,128)S(1)}, u32[]{:S(2)}, u32[]{:S(2)}) collective-permute-start(f32[160,256]{1,0:T(8,128)S(1)} %get-tuple-element.52), channel_id=1, source_target_pairs={{0,248},{8,16},{16,8},{24,32},{32,24},{40,48},{48,40},{56,64},{64,... | collective-permute-start | bytes 491528 | tf_op jit(solution)/shard_map/ppermute | solution.py:458
  16.9 6.0 %collective-permute-start.3 = (f32[160,256]{1,0:T(8,128)S(1)}, f32[160,256]{1,0:T(8,128)S(1)}, u32[]{:S(2)}, u32[]{:S(2)}) collective-permute-start(f32[160,256]{1,0:T(8,128)S(1)} %get-tuple-element.53), channel_id=1, source_target_pairs={{0,8},{8,0},{16,24},{24,16},{32,40},{40,32},{48,56},{56,48},{64,72... | collective-permute-start | bytes 491528 | tf_op jit(solution)/shard_map/ppermute | solution.py:457
  24.3 6.3 %collective-permute-start.4 = (f32[144,256]{1,0:T(8,128)S(1)}, f32[144,256]{1,0:T(8,128)S(1)}, u32[]{:S(2)}, u32[]{:S(2)}) collective-permute-start(f32[144,256]{1,0:T(8,128)S(1)} %get-tuple-element.59), channel_id=1, source_target_pairs={{0,7},{1,2},{2,1},{3,4},{4,3},{5,6},{6,5},{7,0},{8,15},{9,10},{10,... | collective-permute-start | bytes 442376 | tf_op jit(solution)/shard_map/ppermute | solution.py:458
  25.5 7.9 %collective-permute-start.5 = (f32[144,256]{1,0:T(8,128)S(1)}, f32[144,256]{1,0:T(8,128)S(1)}, u32[]{:S(2)}, u32[]{:S(2)}) collective-permute-start(f32[144,256]{1,0:T(8,128)S(1)} %get-tuple-element.60), channel_id=1, source_target_pairs={{0,1},{1,0},{2,3},{3,2},{4,5},{5,4},{6,7},{7,6},{8,9},{9,8},{10,11... | collective-permute-start | bytes 442376 | tf_op jit(solution)/shard_map/ppermute | solution.py:457
  40.9 8.5 %collective-permute-start.6 = (f32[144,256]{1,0:T(8,128)S(1)}, f32[144,256]{1,0:T(8,128)S(1)}, u32[]{:S(2)}, u32[]{:S(2)}) collective-permute-start(f32[144,256]{1,0:T(8,128)S(1)} %get-tuple-element.76), channel_id=1, source_target_pairs={{0,248},{8,16},{16,8},{24,32},{32,24},{40,48},{48,40},{56,64},{64,... | collective-permute-start | bytes 442376 | tf_op jit(solution)/shard_map/ppermute | solution.py:458
  43.3 7.1 %collective-permute-start.7 = (f32[144,256]{1,0:T(8,128)S(1)}, f32[144,256]{1,0:T(8,128)S(1)}, u32[]{:S(2)}, u32[]{:S(2)}) collective-permute-start(f32[144,256]{1,0:T(8,128)S(1)} %get-tuple-element.77), channel_id=1, source_target_pairs={{0,8},{8,0},{16,24},{24,16},{32,40},{40,32},{48,56},{56,48},{64,72... | collective-permute-start | bytes 442376 | tf_op jit(solution)/shard_map/ppermute | solution.py:457
  51.8 6.5 %collective-permute-start.8 = (f32[144,256]{1,0:T(8,128)S(1)}, f32[144,256]{1,0:T(8,128)S(1)}, u32[]{:S(2)}, u32[]{:S(2)}) collective-permute-start(f32[144,256]{1,0:T(8,128)S(1)} %get-tuple-element.81), channel_id=1, source_target_pairs={{0,7},{1,2},{2,1},{3,4},{4,3},{5,6},{6,5},{7,0},{8,15},{9,10},{10,... | collective-permute-start | bytes 442376 | tf_op jit(solution)/shard_map/ppermute | solution.py:458
  53.3 8.0 %collective-permute-start.9 = (f32[144,256]{1,0:T(8,128)S(1)}, f32[144,256]{1,0:T(8,128)S(1)}, u32[]{:S(2)}, u32[]{:S(2)}) collective-permute-start(f32[144,256]{1,0:T(8,128)S(1)} %get-tuple-element.82), channel_id=1, source_target_pairs={{0,1},{1,0},{2,3},{3,2},{4,5},{5,4},{6,7},{7,6},{8,9},{9,8},{10,11... | collective-permute-start | bytes 442376 | tf_op jit(solution)/shard_map/ppermute | solution.py:457
  64.8 23.7 %all-to-all-start = ((f32[256,1,128]{2,1,0:T(1,128)}), f32[256,1,128]{2,1,0:T(1,128)S(1)}, u32[]{:S(2)}, u32[]{:S(2)}) async-start(f32[256,1,128]{2,1,0:T(1,128)} %bitcast.9), calls=%async_computation | async-start | bytes 262144 | tf_op jit(solution)/shard_map/all_to_all | solution.py:533

commit v3 on v2

--- a/solution.py
+++ b/solution.py
@@ -471,10 +471,11 @@
         scratch = (pltpu.VMEM((E, T), f32), pltpu.VMEM((8, 384), f32))
 
         ends = jnp.concatenate([amplitude[:8], amplitude[T - 8 :]], 0)
-        live = (jnp.arange(n) < counts[0, 0]).astype(f32)
-        cells = [row_cells[0, 0].astype(f32), col_cells[0, 0].astype(f32)]
-        known = [fracs[0, 0, 0], fracs[1, 0, 0], live, targets[0, 0] * live]
-        points = jnp.stack(cells + known + [jnp.zeros_like(live)] * 2)
+        alive = jnp.arange(n) < counts[0, 0]
+        sources = [row_cells[0, 0].astype(f32), col_cells[0, 0].astype(f32)]
+        sources += [fracs[0, 0, 0], fracs[1, 0, 0], jnp.ones((n,), f32), targets[0, 0]]
+        known = [jnp.where(alive, x, 0.0) for x in sources]
+        points = jnp.stack(known + [jnp.zeros((n,), f32)] * 2)
         far_end, near_end = swap(gy, ends, ends)
         bands = call(bands_kernel, (((E, K), bf16),) * 4, (spot, lengthscale), (0, 1))
         x_bands, y_bands = bands[:2], bands[2:]

time: 90.3 us -> 89.5 us (level)
    select_n x0 -> x3, other arithmetic: none -> 1.59 us  [shards(): known = [jnp.where(alive, x, 0.0) for x in sources]]
  transfers between devices with their start and end apart: 11 -> 11, of which waited for: 6 -> 6; matrix products, arithmetic and copies ran while one was open for 3% -> 2% of each run, Pallas kernels for 11% -> 11%
where the time goes in v3:
time: 89.5 us; the launch traced here: 88.9 us
  starting transfers between devices  34.9 us (39%)
  Pallas kernels  24.7 us (28%)
  waiting for transfers between devices  24.5 us (27%)
  between operations  2.06 us (2%)
  other arithmetic  1.67 us (2%)
  local copies, waits for them, and re-layouts  0.92 us (1%)
    pallas_call x9, Pallas kernels, call(): pl.pallas_call(kernel, out_shape=shapes, in_specs=[smem if i in scalars e...  24.7 us
    ppermute x5, starting transfers between devices, swap(): far = lax.ppermute(far, axis, far_to)  13 us
    all_to_all x1, waiting for transfers between devices, shards(): parts = lax.all_to_all(sums.reshape(devices, 1, 128), (gx, gy), 0, 0)  12.6 us
    ppermute x5, starting transfers between devices, swap(): near = lax.ppermute(near, axis, near_to)  11.4 us
    all_to_all x1, starting transfers between devices, shards(): parts = lax.all_to_all(sums.reshape(devices, 1, 128), (gx, gy), 0, 0)  10.5 us
    ppermute x5, waiting for transfers between devices, swap(): near = lax.ppermute(near, axis, near_to)  6.89 us
    ppermute x5, waiting for transfers between devices, swap(): far = lax.ppermute(far, axis, far_to)  5.11 us
  transfers between devices with their start and end apart: 11, of which 6 were waited for; matrix products, arithmetic and copies ran while one was open for 2% of the time, Pallas kernels for 11%

profile of v3, /device:TPU:1, one launch (start us, length us, event | category | flops | bytes accessed | tf_op | source)
XLA Modules:
  0.0 88.9 jit_solution(10652182489409551609)
XLA Ops:
  0.6 0.7 fusion.1
  1.4 4.3 %collective-permute-start = (f32[16,256]{1,0:T(8,128)S(1)}, f32[16,256]{1,0:T(8,128)S(1)}, u32[]{:S(2)}, u32[]{:S(2)}) collective-permute-start(f32[16,256]{1,0:T(8,128)S(1)} %pad_maximum_fusion), channel_id=1, source_target_pairs={{0,7},{1,2},{2,1},{3,4},{4,3},{5,6},{6,5},{7,0},{8,15},{9,10},{10,... | collective-permute-start | bytes 49160 | tf_op jit(solution)/shard_map/ppermute | solution.py:458
  5.7 0.0 collective-permute-start.1
  6.3 0.8 bitcast_select_fusion.1
  7.2 0.8 bitcast_select_fusion.3
  7.9 0.2 stack.25.points
  8.1 0.0 copy-start
  8.1 0.0 copy-start.1
  8.1 3.7 %shard_map.103 = (f32[264,256]{1,0:T(8,128)S(1)}, f32[8,384]{1,0:T(8,128)S(1)}) custom-call(f32[8,4096]{1,0:T(8,128)S(1)} %stack.25.points), custom_call_target="tpu_custom_call" | custom-call | flops 1610612736 | bytes 1048576 | tf_op jit(solution)/shard_map/pallas_call | solution.py:435
  11.9 0.1 pad_add_fusion.spot
  12.0 0.0 collective-permute-done.far_ends
  12.0 0.0 collective-permute-done.1.near_ends
  12.0 0.0 copy-done
  12.0 0.7 shard_map.104
  12.7 3.5 %collective-permute-start.2 = (f32[160,256]{1,0:T(8,128)S(1)}, f32[160,256]{1,0:T(8,128)S(1)}, u32[]{:S(2)}, u32[]{:S(2)}) collective-permute-start(f32[160,256]{1,0:T(8,128)S(1)} %get-tuple-element.52), channel_id=1, source_target_pairs={{0,248},{8,16},{16,8},{24,32},{32,24},{40,48},{48,40},{56,64},{64,... | collective-permute-start | bytes 491528 | tf_op jit(solution)/shard_map/ppermute | solution.py:458
  16.2 4.8 %collective-permute-start.3 = (f32[160,256]{1,0:T(8,128)S(1)}, f32[160,256]{1,0:T(8,128)S(1)}, u32[]{:S(2)}, u32[]{:S(2)}) collective-permute-start(f32[160,256]{1,0:T(8,128)S(1)} %get-tuple-element.53), channel_id=1, source_target_pairs={{0,8},{8,0},{16,24},{24,16},{32,40},{40,32},{48,56},{56,48},{64,72... | collective-permute-start | bytes 491528 | tf_op jit(solution)/shard_map/ppermute | solution.py:457
  21.1 0.0 copy-done.1
  21.1 1.2 %shard_map.105 = (bf16[264,640]{1,0:T(8,128)(2,1)S(1)}, bf16[264,640]{1,0:T(8,128)(2,1)S(1)}, bf16[264,640]{1,0:T(8,128)(2,1)S(1)}, bf16[264,640]{1,0:T(8,128)(2,1)S(1)}) custom-call(s32[2]{0:T(128)S(1)} %pad_add_fusion.spot, f32[2]{0:T(128)S(1)} %copy-done.1), custom_call_target="tpu_custom_call" | custom-call | bytes 1048576 | tf_op jit(solution)/shard_map/pallas_call | solution.py:435
  22.3 0.0 collective-permute-done.2.far
  22.3 0.0 collective-permute-done.3.near
  22.3 1.3 %shard_map.106 = (f32[256,384]{1,0:T(8,128)S(1)}, f32[8,384]{1,0:T(8,128)S(1)}, f32[8,256]{1,0:T(8,128)S(1)}, f32[144,256]{1,0:T(8,128)S(1)}, f32[144,256]{1,0:T...) custom-call(s32[2]{0:T(128)S(1)} %pad_add_fusion.spot, ...), custom_call_target="tpu_custom_call" | custom-call | bytes 1048576 | tf_op jit(solution)/shard_map/pallas_call | solution.py:435
  23.6 1.2 %collective-permute-start.4 = (f32[144,256]{1,0:T(8,128)S(1)}, f32[144,256]{1,0:T(8,128)S(1)}, u32[]{:S(2)}, u32[]{:S(2)}) collective-permute-start(f32[144,256]{1,0:T(8,128)S(1)} %get-tuple-element.59), channel_id=1, source_target_pairs={{0,7},{1,2},{2,1},{3,4},{4,3},{5,6},{6,5},{7,0},{8,15},{9,10},{10,... | collective-permute-start | bytes 442376 | tf_op jit(solution)/shard_map/ppermute | solution.py:458
  24.9 0.5 collective-permute-start.5
  25.3 4.5 %shard_map.107 = (bf16[256,4096]{1,0:T(8,128)(2,1)S(1)}, bf16[256,4096]{1,0:T(8,128)(2,1)S(1)}, bf16[16,4096]{1,0:T(8,128)(2,1)S(1)}, f32[264,4096]{1,0:T(8,128)...) custom-call(f32[8,4096]{1,0:T(8,128)S(1)} %stack.25.points, ...), custom_call_target="tpu_custom_call" | custom-call | flops 805306368 | bytes 1048576 | tf_op jit(solution)/shard_map/pallas_call | solution.py:435
  29.8 0.1 collective-permute-done.4.far
  29.9 2.9 %collective-permute-done.5.near = f32[144,256]{1,0:T(8,128)S(1)} collective-permute-done((f32[144,256]{1,0:T(8,128)S(1)}, f32[144,256]{1,0:T(8,128)S(1)}, u32[]{:S(2)}, u32[]{:S(2)}) %collective-permute-start.5) | collective-permute-done | bytes 147488 | tf_op jit(solution)/shard_map/ppermute | solution.py:457
  32.8 7.4 %shard_map.108 = (f32[1,4096]{1,0:T(1,128)S(1)}, f32[264,256]{1,0:T(8,128)S(1)}, f32[8,384]{1,0:T(8,128)S(1)}, f32[144,256]{1,0:T(8,128)S(1)}, f32[144,256]{1,0:T(8,128)S(1)}) custom-call(s32[2]{0:T(128)S(1)} %pad_add_fusion.spot, f32[256,384]{1,0:T(8,128)S(1)} %get-tuple-element.56.row, f32[8,384]{1,0:T(8,128)S(1)} %get-tuple-element.57.group, ...), custom_call_target="tpu_custom_call" | custom-call | bytes 1048576 | tf_op jit(solution)/shard_map/pallas_call | solution.py:435
  40.2 2.4 %collective-permute-start.6 = (f32[144,256]{1,0:T(8,128)S(1)}, f32[144,256]{1,0:T(8,128)S(1)}, u32[]{:S(2)}, u32[]{:S(2)}) collective-permute-start(f32[144,256]{1,0:T(8,128)S(1)} %get-tuple-element.76), channel_id=1, source_target_pairs={{0,248},{8,16},{16,8},{24,32},{32,24},{40,48},{48,40},{56,64},{64,... | collective-permute-start | bytes 442376 | tf_op jit(solution)/shard_map/ppermute | solution.py:458
  42.6 6.1 %collective-permute-start.7 = (f32[144,256]{1,0:T(8,128)S(1)}, f32[144,256]{1,0:T(8,128)S(1)}, u32[]{:S(2)}, u32[]{:S(2)}) collective-permute-start(f32[144,256]{1,0:T(8,128)S(1)} %get-tuple-element.77), channel_id=1, source_target_pairs={{0,8},{8,0},{16,24},{24,16},{32,40},{40,32},{48,56},{56,48},{64,72... | collective-permute-start | bytes 442376 | tf_op jit(solution)/shard_map/ppermute | solution.py:457
  48.7 0.0 collective-permute-done.6.far
  48.7 1.0 %collective-permute-done.7.near = f32[144,256]{1,0:T(8,128)S(1)} collective-permute-done((f32[144,256]{1,0:T(8,128)S(1)}, f32[144,256]{1,0:T(8,128)S(1)}, u32[]{:S(2)}, u32[]{:S(2)}) %collective-permute-start.7) | collective-permute-done | bytes 147488 | tf_op jit(solution)/shard_map/ppermute | solution.py:457
  49.7 1.3 %shard_map.109 = (f32[256,384]{1,0:T(8,128)S(1)}, f32[8,384]{1,0:T(8,128)S(1)}, f32[8,256]{1,0:T(8,128)S(1)}, f32[144,256]{1,0:T(8,128)S(1)}, f32[144,256]{1,0:T(8,128)S(1)}) custom-call(s32[2]{0:T(128)S(1)} %pad_add_fusion.spot, f32[264,256]{1,0:T(8,128)S(1)} %get-tuple-element.73.main, f32[8,384]{1,0:T(8,128)S(1)} %get-tuple-element.74.edge, ...), custom_call_target="tpu_custom_call" | custom-call | bytes 1048576 | tf_op jit(solution)/shard_map/pallas_call | solution.py:435
  51.1 1.5 %collective-permute-start.8 = (f32[144,256]{1,0:T(8,128)S(1)}, f32[144,256]{1,0:T(8,128)S(1)}, u32[]{:S(2)}, u32[]{:S(2)}) collective-permute-start(f32[144,256]{1,0:T(8,128)S(1)} %get-tuple-element.81), channel_id=1, source_target_pairs={{0,7},{1,2},{2,1},{3,4},{4,3},{5,6},{6,5},{7,0},{8,15},{9,10},{10,... | collective-permute-start | bytes 442376 | tf_op jit(solution)/shard_map/ppermute | solution.py:458
  52.6 0.0 collective-permute-start.9
  52.6 5.0 %collective-permute-done.8.far = f32[144,256]{1,0:T(8,128)S(1)} collective-permute-done((f32[144,256]{1,0:T(8,128)S(1)}, f32[144,256]{1,0:T(8,128)S(1)}, u32[]{:S(2)}, u32[]{:S(2)}) %collective-permute-start.8) | collective-permute-done | bytes 147488 | tf_op jit(solution)/shard_map/ppermute | solution.py:458
  57.6 3.0 %collective-permute-done.9.near = f32[144,256]{1,0:T(8,128)S(1)} collective-permute-done((f32[144,256]{1,0:T(8,128)S(1)}, f32[144,256]{1,0:T(8,128)S(1)}, u32[]{:S(2)}, u32[]{:S(2)}) %collective-permute-start.9) | collective-permute-done | bytes 147488 | tf_op jit(solution)/shard_map/ppermute | solution.py:457
  60.6 3.6 %shard_map.110 = (f32[1,4096]{1,0:T(1,128)S(1)}, f32[256,128]{1,0:T(8,128)}) custom-call(f32[256,384]{1,0:T(8,128)S(1)} %get-tuple-element.78.row, f32[8,384]{1,0:T(8,128)S(1)} %get-tuple-element.79.group, f32[8,256]{1,0:T(8,128)S(1)} %get-tuple-element.80.tail, f32[144,256]{1,0:T(8,128)S(1)} %collective-permute-done.8.far, ...), custom_call_target="tpu_custom_call" | custom-call | bytes 1048576 | tf_op jit(solution)/shard_map/pallas_call | solution.py:435
  64.2 10.5 %all-to-all-start = ((f32[256,1,128]{2,1,0:T(1,128)}), f32[256,1,128]{2,1,0:T(1,128)S(1)}, u32[]{:S(2)}, u32[]{:S(2)}) async-start(f32[256,1,128]{2,1,0:T(1,128)} %bitcast.9), calls=%async_computation | async-start | bytes 262144 | tf_op jit(solution)/shard_map/all_to_all | solution.py:534
  75.4 12.6 %all-to-all-done = f32[256,1,128]{2,1,0:T(1,128)S(1)} async-done(((f32[256,1,128]{2,1,0:T(1,128)}), f32[256,1,128]{2,1,0:T(1,128)S(1)}, u32[]{:S(2)}, u32[]{:S(2)}) %all-to-all-start) | async-done | bytes 131104 | tf_op jit(solution)/shard_map/all_to_all | solution.py:534
  87.9 0.9 %shard_map.111 = (f32[1,4096]{1,0:T(1,128)}, f32[1,4096]{1,0:T(1,128)}, f32[1,128]{1,0:T(1,128)}) custom-call(f32[1]{0:T(128)S(6)} %copy.13.ridge, f32[256,128]{1,0:T(8,128)S(1)} %bitcast.24, f32[8,4096]{1,0:T(8,128)S(1)} %stack.25.points, f32[1,4096]{1,0:T(1,128)S(1)} %get-tuple-element.83.image, f32[1,4096]{1,0:T(1,128)S(1)} %get-tuple-element.85.image_two), custom_call_target="tpu_custom_call" | custom-call | bytes 1048576 | tf_op jit(solution)/shard_map/pallas_call | solution.py:435
  (3 shorter events, 0.0 us)
Async XLA Ops:
  1.4 10.6 %collective-permute-start = (f32[16,256]{1,0:T(8,128)S(1)}, f32[16,256]{1,0:T(8,128)S(1)}, u32[]{:S(2)}, u32[]{:S(2)}) collective-permute-start(f32[16,256]{1,0:T(8,128)S(1)} %pad_maximum_fusion), channel_id=1, source_target_pairs={{0,7},{1,2},{2,1},{3,4},{4,3},{5,6},{6,5},{7,0},{8,15},{9,10},{10,... | collective-permute-start | bytes 49160 | tf_op jit(solution)/shard_map/ppermute | solution.py:458
  5.7 6.3 %collective-permute-start.1 = (f32[16,256]{1,0:T(8,128)S(1)}, f32[16,256]{1,0:T(8,128)S(1)}, u32[]{:S(2)}, u32[]{:S(2)}) collective-permute-start(f32[16,256]{1,0:T(8,128)S(1)} %pad_maximum_fusion), channel_id=1, source_target_pairs={{0,1},{1,0},{2,3},{3,2},{4,5},{5,4},{6,7},{7,6},{8,9},{9,8},{10,11... | collective-permute-start | bytes 49160 | tf_op jit(solution)/shard_map/ppermute | solution.py:457
  8.1 3.8 %copy-start = (f32[256,256]{1,0:T(8,128)S(1)}, f32[256,256]{1,0:T(8,128)}, u32[]{:S(2)}) copy-start(f32[256,256]{1,0:T(8,128)} %amplitude.3) | copy-start | bytes 786436
  8.1 13.0 %copy-start.1 = (f32[2]{0:T(128)S(1)}, f32[2]{0:T(128)}, u32[]{:S(2)}) copy-start(f32[2]{0:T(128)} %scales.1) | copy-start | bytes 28
  12.7 9.6 %collective-permute-start.2 = (f32[160,256]{1,0:T(8,128)S(1)}, f32[160,256]{1,0:T(8,128)S(1)}, u32[]{:S(2)}, u32[]{:S(2)}) collective-permute-start(f32[160,256]{1,0:T(8,128)S(1)} %get-tuple-element.52), channel_id=1, source_target_pairs={{0,248},{8,16},{16,8},{24,32},{32,24},{40,48},{48,40},{56,64},{64,... | collective-permute-start | bytes 491528 | tf_op jit(solution)/shard_map/ppermute | solution.py:458
  16.2 6.0 %collective-permute-start.3 = (f32[160,256]{1,0:T(8,128)S(1)}, f32[160,256]{1,0:T(8,128)S(1)}, u32[]{:S(2)}, u32[]{:S(2)}) collective-permute-start(f32[160,256]{1,0:T(8,128)S(1)} %get-tuple-element.53), channel_id=1, source_target_pairs={{0,8},{8,0},{16,24},{24,16},{32,40},{40,32},{48,56},{56,48},{64,72... | collective-permute-start | bytes 491528 | tf_op jit(solution)/shard_map/ppermute | solution.py:457
  23.6 6.3 %collective-permute-start.4 = (f32[144,256]{1,0:T(8,128)S(1)}, f32[144,256]{1,0:T(8,128)S(1)}, u32[]{:S(2)}, u32[]{:S(2)}) collective-permute-start(f32[144,256]{1,0:T(8,128)S(1)} %get-tuple-element.59), channel_id=1, source_target_pairs={{0,7},{1,2},{2,1},{3,4},{4,3},{5,6},{6,5},{7,0},{8,15},{9,10},{10,... | collective-permute-start | bytes 442376 | tf_op jit(solution)/shard_map/ppermute | solution.py:458
  24.9 7.9 %collective-permute-start.5 = (f32[144,256]{1,0:T(8,128)S(1)}, f32[144,256]{1,0:T(8,128)S(1)}, u32[]{:S(2)}, u32[]{:S(2)}) collective-permute-start(f32[144,256]{1,0:T(8,128)S(1)} %get-tuple-element.60), channel_id=1, source_target_pairs={{0,1},{1,0},{2,3},{3,2},{4,5},{5,4},{6,7},{7,6},{8,9},{9,8},{10,11... | collective-permute-start | bytes 442376 | tf_op jit(solution)/shard_map/ppermute | solution.py:457
  40.2 8.5 %collective-permute-start.6 = (f32[144,256]{1,0:T(8,128)S(1)}, f32[144,256]{1,0:T(8,128)S(1)}, u32[]{:S(2)}, u32[]{:S(2)}) collective-permute-start(f32[144,256]{1,0:T(8,128)S(1)} %get-tuple-element.76), channel_id=1, source_target_pairs={{0,248},{8,16},{16,8},{24,32},{32,24},{40,48},{48,40},{56,64},{64,... | collective-permute-start | bytes 442376 | tf_op jit(solution)/shard_map/ppermute | solution.py:458
  42.6 7.1 %collective-permute-start.7 = (f32[144,256]{1,0:T(8,128)S(1)}, f32[144,256]{1,0:T(8,128)S(1)}, u32[]{:S(2)}, u32[]{:S(2)}) collective-permute-start(f32[144,256]{1,0:T(8,128)S(1)} %get-tuple-element.77), channel_id=1, source_target_pairs={{0,8},{8,0},{16,24},{24,16},{32,40},{40,32},{48,56},{56,48},{64,72... | collective-permute-start | bytes 442376 | tf_op jit(solution)/shard_map/ppermute | solution.py:457
  51.1 6.5 %collective-permute-start.8 = (f32[144,256]{1,0:T(8,128)S(1)}, f32[144,256]{1,0:T(8,128)S(1)}, u32[]{:S(2)}, u32[]{:S(2)}) collective-permute-start(f32[144,256]{1,0:T(8,128)S(1)} %get-tuple-element.81), channel_id=1, source_target_pairs={{0,7},{1,2},{2,1},{3,4},{4,3},{5,6},{6,5},{7,0},{8,15},{9,10},{10,... | collective-permute-start | bytes 442376 | tf_op jit(solution)/shard_map/ppermute | solution.py:458
  52.6 8.0 %collective-permute-start.9 = (f32[144,256]{1,0:T(8,128)S(1)}, f32[144,256]{1,0:T(8,128)S(1)}, u32[]{:S(2)}, u32[]{:S(2)}) collective-permute-start(f32[144,256]{1,0:T(8,128)S(1)} %get-tuple-element.82), channel_id=1, source_target_pairs={{0,1},{1,0},{2,3},{3,2},{4,5},{5,4},{6,7},{7,6},{8,9},{9,8},{10,11... | collective-permute-start | bytes 442376 | tf_op jit(solution)/shard_map/ppermute | solution.py:457
  64.2 23.7 %all-to-all-start = ((f32[256,1,128]{2,1,0:T(1,128)}), f32[256,1,128]{2,1,0:T(1,128)S(1)}, u32[]{:S(2)}, u32[]{:S(2)}) async-start(f32[256,1,128]{2,1,0:T(1,128)} %bitcast.9), calls=%async_computation | async-start | bytes 262144 | tf_op jit(solution)/shard_map/all_to_all | solution.py:534
